TPU v7x, 32 devices: a whole 2x2x4 slice. The times are simulated.
32 devices in a mesh: dp: 16 (over z, y, x), tensor: 2 (over core).
Axes of the slice: x: 2, y: 2, z: 4, core: 2. Of those that a mesh axis runs over, the one named last changes fastest.
Arguments:
- tokens: bfloat16 [4096, 1024], P('dp'), may hold values from -6 to 6
- encoder_states: bfloat16 [4096, 1024], P('dp'), may hold values from -6 to 6
- cotangent: bfloat16 [4096, 1024], P('dp'), may hold values from -6 to 6
- lengths: int32 [16], replicated, may hold values from 1 to 256, 3686 in all
- deal_order: int32 [16], replicated, may hold values from 0 to 15, each once
- bucket_index: int32 [256], replicated, may hold values from 0 to 31, as said below
- rel_table: float32 [32, 16], P(None, 'tensor'), may hold values from -4 to 4
- gain_self: float32 [1024], replicated, may hold values from 0.5 to 1.5
- self_query: bfloat16 [1024, 1024], P('dp', 'tensor'), may hold values from -0.046875 to 0.046875
- self_key: bfloat16 [1024, 1024], P('dp', 'tensor'), may hold values from -0.1875 to 0.1875
- self_value: bfloat16 [1024, 1024], P('dp', 'tensor'), may hold values from -0.1875 to 0.1875
- self_output: bfloat16 [1024, 1024], P('dp', 'tensor'), may hold values from -0.75 to 0.75
- gain_cross: float32 [1024], replicated, may hold values from 0.5 to 1.5
- cross_query: bfloat16 [1024, 1024], P('dp', 'tensor'), may hold values from -0.046875 to 0.046875
- cross_key: bfloat16 [1024, 1024], P('dp', 'tensor'), may hold values from -0.1875 to 0.1875
- cross_value: bfloat16 [1024, 1024], P('dp', 'tensor'), may hold values from -0.1875 to 0.1875
- cross_output: bfloat16 [1024, 1024], P('dp', 'tensor'), may hold values from -0.75 to 0.75
- gain_feed: float32 [1024], replicated, may hold values from 0.5 to 1.5
- feed_gate: bfloat16 [1024, 2816], P('dp', 'tensor'), may hold values from -0.1875 to 0.1875
- feed_value: bfloat16 [1024, 2816], P('dp', 'tensor'), may hold values from -0.1875 to 0.1875
- feed_output: bfloat16 [1024, 2816], P('dp', 'tensor'), may hold values from -0.109375 to 0.109375
Outputs:
- layer_out: bfloat16 [4096, 1024], P('dp')
- tokens_grad: bfloat16 [4096, 1024], P('dp')
- encoder_grad: bfloat16 [4096, 1024], P(('dp', 'tensor'))
- rel_table_grad: float32 [32, 16], P(None, 'tensor')
- gain_self_grad: float32 [1024], replicated
- self_query_grad: float32 [1024, 1024], P('dp', 'tensor')
- self_key_grad: float32 [1024, 1024], P('dp', 'tensor')
- self_value_grad: float32 [1024, 1024], P('dp', 'tensor')
- self_output_grad: float32 [1024, 1024], P('dp', 'tensor')
- gain_cross_grad: float32 [1024], replicated
- cross_query_grad: float32 [1024, 1024], P('dp', 'tensor')
- cross_key_grad: float32 [1024, 1024], P('dp', 'tensor')
- cross_value_grad: float32 [1024, 1024], P('dp', 'tensor')
- cross_output_grad: float32 [1024, 1024], P('dp', 'tensor')
- gain_feed_grad: float32 [1024], replicated
- feed_gate_grad: float32 [1024, 2816], P('dp', 'tensor')
- feed_value_grad: float32 [1024, 2816], P('dp', 'tensor')
- feed_output_grad: float32 [1024, 2816], P('dp', 'tensor')
Inputs may be any that keep to these rules, and one draw needn't show every extreme that they name: `lengths`: one sequence has exactly 256 tokens. `deal_order`: each dp index receives exactly one sequence. `bucket_index`: never falls as the distance grows; distance 0 has bucket 0 and distance 256 - 1 has bucket 32 - 1.
All inputs are finite; a program needn't handle non-finite values.
Results may differ from a plain program's by a relative error of at most 0.04.
Values may be sent and summed in bfloat16 or wider, within the bound.
No kernel may reach another device: no remote copies, remote signals or barrier semaphores. Data moves between devices by JAX's collectives and lax.ppermute only.
A program may use at most 192 MiB of HBM per device.

v0:
```python
import jax
import jax.numpy as jnp
from jax import lax
from jax.sharding import PartitionSpec as P

LEN = 256


EPSILON = 1e-06
MASKED = -1e30
HIGHEST = lax.Precision.HIGHEST


def product_plain(left, right):
    return jnp.dot(left, right, preferred_element_type=jnp.float32)


def product_right(left, right):
    return lax.dot_general(
        left, right, (((1,), (1,)), ((), ())), preferred_element_type=jnp.float32
    )


def product_left(left, right):
    return lax.dot_general(
        left, right, (((0,), (0,)), ((), ())), preferred_element_type=jnp.float32
    )


def norm_forward(activation, gain_in):
    inv_root = lax.rsqrt(jnp.mean(activation * activation, axis=-1, keepdims=True) + EPSILON)
    return (activation * inv_root * gain_in, inv_root)


def norm_backward(activation, inv_root, gain_in, upstream):
    weighted = upstream * gain_in
    inner_mean = jnp.mean(weighted * activation, axis=-1, keepdims=True)
    grad_in = inv_root * weighted - activation * (inv_root * inv_root * inv_root) * inner_mean
    return (grad_in, jnp.sum(upstream * activation * inv_root, axis=0))


def split_heads(activation, head_count):
    return activation.reshape(activation.shape[0], head_count, -1)


def head_scores(query_part, key_part, head_count):
    return jnp.einsum(
        "qhe,khe->hqk",
        split_heads(query_part, head_count),
        split_heads(key_part, head_count),
        preferred_element_type=jnp.float32,
    )


def softmax_forward(scores, value_part, head_count):
    highest = jnp.max(scores, axis=-1, keepdims=True)
    exponent = jnp.exp(scores - highest)
    totals = jnp.sum(exponent, axis=-1, keepdims=True)
    weights_low = (exponent / totals).astype(jnp.bfloat16)
    mixed_out = jnp.einsum(
        "hqk,khe->qhe",
        weights_low,
        split_heads(value_part, head_count),
        preferred_element_type=jnp.float32,
    )
    return (mixed_out.reshape(mixed_out.shape[0], -1), highest[..., 0] + jnp.log(totals[..., 0]))


def softmax_backward(scores, log_total, query_part, key_part, value_part, upstream, head_count):
    chance = jnp.exp(scores - log_total[..., None])
    upstream_heads = split_heads(upstream, head_count)
    chance_grad = jnp.einsum(
        "qhe,khe->hqk",
        upstream_heads,
        split_heads(value_part, head_count),
        preferred_element_type=jnp.float32,
    )
    row_delta = jnp.sum(chance * chance_grad, axis=-1, keepdims=True)
    score_grad = (chance * (chance_grad - row_delta)).astype(jnp.bfloat16)
    query_grad = jnp.einsum(
        "hqk,khe->qhe",
        score_grad,
        split_heads(key_part, head_count),
        preferred_element_type=jnp.float32,
    )
    key_grad = jnp.einsum(
        "hqk,qhe->khe",
        score_grad,
        split_heads(query_part, head_count),
        preferred_element_type=jnp.float32,
    )
    value_grad = jnp.einsum(
        "hqk,qhe->khe",
        chance.astype(jnp.bfloat16),
        upstream_heads,
        preferred_element_type=jnp.float32,
    )
    return (
        query_grad.reshape(query_grad.shape[0], -1),
        key_grad.reshape(key_grad.shape[0], -1),
        value_grad.reshape(value_grad.shape[0], -1),
        score_grad,
    )


def self_block_scores(query_self, key_self, distance_bias, positions, my_length, head_count):
    raw_scores = head_scores(query_self, key_self, head_count)
    distance = jnp.clip(positions[:, None] - positions[None, :], 0, positions.shape[0] - 1)
    raw_scores = raw_scores + jnp.take(distance_bias, distance, axis=1)
    allowed = (positions[None, :] <= positions[:, None]) & (positions[None, :] < my_length)
    return jnp.where(allowed[None], raw_scores, MASKED)


def diagonal_sums(score_part):
    head_count, block_rows, _ = score_part.shape
    flipped = score_part[:, :, ::-1]
    padded = jnp.pad(flipped, ((0, 0), (0, 0), (0, block_rows)))
    flat = padded.reshape(head_count, block_rows * 2 * block_rows)[
        :, : block_rows * (2 * block_rows - 1)
    ]
    skewed = flat.reshape(head_count, block_rows, 2 * block_rows - 1)
    return jnp.sum(skewed, axis=1, dtype=jnp.float32)


def gelu_product(gate_pre, lift_pre):
    return jax.nn.gelu(gate_pre, approximate=True) * lift_pre


def branch_total(partial_value):
    return lax.psum(partial_value.astype(jnp.bfloat16), "tensor").astype(jnp.float32)


def input_total(partial_value):
    return lax.psum(partial_value.astype(jnp.bfloat16), "tensor").astype(jnp.float32)


def on_device(
    tokens,
    encoder_states,
    cotangent,
    lengths,
    deal_order,
    bucket_index,
    rel_table,
    gain_self,
    self_query,
    self_key,
    self_value,
    self_output,
    gain_cross,
    cross_query,
    cross_key,
    cross_value,
    cross_output,
    gain_feed,
    feed_gate,
    feed_value,
    feed_output,
):
    devices = lax.axis_size("dp")
    myself = lax.axis_index("dp")
    head_count = rel_table.shape[1]
    model_width = tokens.shape[1]
    piece_rows = LEN // devices
    block_rows = min(512, LEN)
    numbers = jnp.arange(devices, dtype=jnp.int32)
    owner_of = jnp.sum(
        jnp.where(deal_order[:, None] == numbers[None, :], numbers[:, None], 0), axis=0
    )
    my_length = jnp.sum(jnp.where(deal_order == myself, lengths, 0))
    first_step = (
        lax.all_to_all(
            tokens.reshape(devices, piece_rows, model_width),
            "dp",
            split_axis=0,
            concat_axis=0,
            tiled=True,
        ),
        lax.all_to_all(
            cotangent.reshape(devices, piece_rows, model_width),
            "dp",
            split_axis=0,
            concat_axis=0,
            tiled=True,
        ),
    )
    second_step = (
        lax.all_to_all(
            jnp.take(first_step[0], owner_of, axis=0), "dp", split_axis=0, concat_axis=0, tiled=True
        ),
        lax.all_to_all(
            jnp.take(first_step[1], owner_of, axis=0), "dp", split_axis=0, concat_axis=0, tiled=True
        ),
    )
    source = second_step[0].reshape(LEN, model_width)
    upstream_out = second_step[1].reshape(LEN, model_width)
    gathered = (
        lax.all_gather(self_query, "dp", axis=0, tiled=True),
        lax.all_gather(self_key, "dp", axis=0, tiled=True),
        lax.all_gather(self_value, "dp", axis=0, tiled=True),
        lax.all_gather(self_output, "dp", axis=0, tiled=True),
        lax.all_gather(cross_query, "dp", axis=0, tiled=True),
        lax.all_gather(cross_key, "dp", axis=0, tiled=True),
        lax.all_gather(cross_value, "dp", axis=0, tiled=True),
        lax.all_gather(cross_output, "dp", axis=0, tiled=True),
        lax.all_gather(feed_gate, "dp", axis=0, tiled=True),
        lax.all_gather(feed_value, "dp", axis=0, tiled=True),
        lax.all_gather(feed_output, "dp", axis=0, tiled=True),
    )
    (
        query_weight,
        key_weight,
        value_weight,
        output_weight,
        cross_query_weight,
        cross_key_weight,
        cross_value_weight,
        cross_output_weight,
        gate_weight,
        lift_weight,
        down_weight,
    ) = gathered
    positions = jnp.arange(LEN, dtype=jnp.int32)
    valid_rows = (positions < my_length).astype(jnp.float32)[:, None]
    onehot_bucket = (
        bucket_index[:, None] == jnp.arange(rel_table.shape[0], dtype=jnp.int32)[None, :]
    ).astype(jnp.float32)
    distance_bias = jnp.dot(onehot_bucket, rel_table, precision=HIGHEST).T
    masked_input = source.astype(jnp.float32) * valid_rows
    normed_self, root_self = norm_forward(masked_input, gain_self)
    normed_self_low = normed_self.astype(jnp.bfloat16)
    query_self = product_plain(normed_self_low, query_weight).astype(jnp.bfloat16)
    key_self = product_plain(normed_self_low, key_weight).astype(jnp.bfloat16)
    value_self = product_plain(normed_self_low, value_weight).astype(jnp.bfloat16)
    scores = self_block_scores(
        query_self, key_self, distance_bias, positions, my_length, head_count
    )
    mixed_out, log_total = softmax_forward(scores, value_self, head_count)
    self_parts = mixed_out
    self_logs = [log_total]
    self_mixed_low = self_parts.astype(jnp.bfloat16)
    hidden_one = masked_input + branch_total(product_right(self_mixed_low, output_weight))
    normed_cross, root_cross = norm_forward(hidden_one, gain_cross)
    normed_cross_low = normed_cross.astype(jnp.bfloat16)
    query_cross = product_plain(normed_cross_low, cross_query_weight).astype(jnp.bfloat16)
    key_cross = product_plain(encoder_states, cross_key_weight).astype(jnp.bfloat16)
    value_cross = product_plain(encoder_states, cross_value_weight).astype(jnp.bfloat16)
    scores = head_scores(query_cross, key_cross, head_count)
    mixed_out, log_total = softmax_forward(scores, value_cross, head_count)
    cross_logs = [log_total]
    cross_mixed_low = mixed_out.astype(jnp.bfloat16)
    hidden_two = hidden_one + branch_total(product_right(cross_mixed_low, cross_output_weight))
    normed_feed, root_feed = norm_forward(hidden_two, gain_feed)
    normed_feed_low = normed_feed.astype(jnp.bfloat16)
    gate_pre = product_plain(normed_feed_low, gate_weight)
    lift_pre = product_plain(normed_feed_low, lift_weight)
    hidden_low = gelu_product(gate_pre, lift_pre).astype(jnp.bfloat16)
    hidden_three = hidden_two + branch_total(product_right(hidden_low, down_weight))
    layer_result = (hidden_three * valid_rows).astype(jnp.bfloat16)
    (
        query_weight,
        key_weight,
        value_weight,
        output_weight,
        cross_query_weight,
        cross_key_weight,
        cross_value_weight,
        cross_output_weight,
        gate_weight,
        lift_weight,
        down_weight,
    ) = gathered
    grad_three = upstream_out.astype(jnp.float32) * valid_rows
    branch_grad = grad_three.astype(jnp.bfloat16)
    down_weight_grad = product_left(branch_grad, hidden_low)
    hidden_grad = product_plain(branch_grad, down_weight)
    gate_grad, lift_grad = jax.vjp(gelu_product, gate_pre, lift_pre)[1](hidden_grad)
    gate_grad_low = gate_grad.astype(jnp.bfloat16)
    lift_grad_low = lift_grad.astype(jnp.bfloat16)
    gate_weight_grad = product_left(normed_feed_low, gate_grad_low)
    lift_weight_grad = product_left(normed_feed_low, lift_grad_low)
    feed_normed_grad = input_total(
        product_right(gate_grad_low, gate_weight) + product_right(lift_grad_low, lift_weight)
    )
    back_feed, gain_feed_grad = norm_backward(hidden_two, root_feed, gain_feed, feed_normed_grad)
    grad_two = grad_three + back_feed
    branch_grad = grad_two.astype(jnp.bfloat16)
    cross_output_grad = product_left(branch_grad, cross_mixed_low)
    mixed_grad = product_plain(branch_grad, cross_output_weight).astype(jnp.bfloat16)
    query_parts = []
    number = 0
    scores = head_scores(query_cross, key_cross, head_count)
    query_grad, key_grad, value_grad, _ = softmax_backward(
        scores, cross_logs[number], query_cross, key_cross, value_cross, mixed_grad, head_count
    )
    query_parts.append(query_grad)
    key_running = key_grad
    value_running = value_grad
    query_grad_low = query_parts[0].astype(jnp.bfloat16)
    key_grad_low = key_running.astype(jnp.bfloat16)
    value_grad_low = value_running.astype(jnp.bfloat16)
    cross_query_grad = product_left(normed_cross_low, query_grad_low)
    cross_key_grad = product_left(encoder_states, key_grad_low)
    cross_value_grad = product_left(encoder_states, value_grad_low)
    encoder_partial = product_right(key_grad_low, cross_key_weight) + product_right(
        value_grad_low, cross_value_weight
    )
    encoder_grad = lax.psum_scatter(
        encoder_partial.astype(jnp.bfloat16), "tensor", scatter_dimension=0, tiled=True
    )
    cross_normed_grad = input_total(product_right(query_grad_low, cross_query_weight))
    back_cross, gain_cross_grad = norm_backward(
        hidden_one, root_cross, gain_cross, cross_normed_grad
    )
    grad_one = grad_two + back_cross
    upper_sums = (
        lax.psum_scatter(cross_query_grad, "dp", scatter_dimension=0, tiled=True),
        lax.psum_scatter(cross_key_grad, "dp", scatter_dimension=0, tiled=True),
        lax.psum_scatter(cross_value_grad, "dp", scatter_dimension=0, tiled=True),
        lax.psum_scatter(cross_output_grad, "dp", scatter_dimension=0, tiled=True),
        lax.psum_scatter(gate_weight_grad, "dp", scatter_dimension=0, tiled=True),
        lax.psum_scatter(lift_weight_grad, "dp", scatter_dimension=0, tiled=True),
        lax.psum_scatter(down_weight_grad, "dp", scatter_dimension=0, tiled=True),
    )
    branch_grad = grad_one.astype(jnp.bfloat16)
    output_weight_grad = product_left(branch_grad, self_mixed_low)
    mixed_grad = product_plain(branch_grad, output_weight).astype(jnp.bfloat16)
    query_parts = []
    distance_grad = jnp.zeros((head_count, LEN), jnp.float32)
    number = 0
    scores = self_block_scores(
        query_self, key_self, distance_bias, positions, my_length, head_count
    )
    query_grad, key_grad, value_grad, score_grad = softmax_backward(
        scores, self_logs[number], query_self, key_self, value_self, mixed_grad, head_count
    )
    query_parts.append(query_grad)
    diagonal = diagonal_sums(score_grad)
    distance_grad = distance_grad.at[:, :block_rows].add(diagonal[:, block_rows - 1 :])
    table_grad = jnp.dot(onehot_bucket.T, distance_grad.T, precision=HIGHEST)
    query_grad_low = query_parts[0].astype(jnp.bfloat16)
    key_grad_low = key_grad.astype(jnp.bfloat16)
    value_grad_low = value_grad.astype(jnp.bfloat16)
    query_weight_grad = product_left(normed_self_low, query_grad_low)
    key_weight_grad = product_left(normed_self_low, key_grad_low)
    value_weight_grad = product_left(normed_self_low, value_grad_low)
    self_normed_grad = input_total(
        product_right(query_grad_low, query_weight)
        + product_right(key_grad_low, key_weight)
        + product_right(value_grad_low, value_weight)
    )
    back_self, gain_self_grad = norm_backward(masked_input, root_self, gain_self, self_normed_grad)
    input_grad = ((grad_one + back_self) * valid_rows).astype(jnp.bfloat16)
    lower_sums = (
        lax.psum_scatter(query_weight_grad, "dp", scatter_dimension=0, tiled=True),
        lax.psum_scatter(key_weight_grad, "dp", scatter_dimension=0, tiled=True),
        lax.psum_scatter(value_weight_grad, "dp", scatter_dimension=0, tiled=True),
        lax.psum_scatter(output_weight_grad, "dp", scatter_dimension=0, tiled=True),
    )
    weight_sums = lower_sums + upper_sums
    small_sums = lax.psum((table_grad, gain_self_grad, gain_cross_grad, gain_feed_grad), "dp")
    back_first = (
        lax.all_to_all(
            layer_result.reshape(devices, piece_rows, model_width),
            "dp",
            split_axis=0,
            concat_axis=0,
            tiled=True,
        ),
        lax.all_to_all(
            input_grad.reshape(devices, piece_rows, model_width),
            "dp",
            split_axis=0,
            concat_axis=0,
            tiled=True,
        ),
    )
    back_second = (
        lax.all_to_all(
            jnp.take(back_first[0], deal_order, axis=0),
            "dp",
            split_axis=0,
            concat_axis=0,
            tiled=True,
        ),
        lax.all_to_all(
            jnp.take(back_first[1], deal_order, axis=0),
            "dp",
            split_axis=0,
            concat_axis=0,
            tiled=True,
        ),
    )
    return (
        back_second[0].reshape(LEN, model_width),
        back_second[1].reshape(LEN, model_width),
        encoder_grad,
        small_sums[0],
        small_sums[1],
        weight_sums[0],
        weight_sums[1],
        weight_sums[2],
        weight_sums[3],
        small_sums[2],
        weight_sums[4],
        weight_sums[5],
        weight_sums[6],
        weight_sums[7],
        small_sums[3],
        weight_sums[8],
        weight_sums[9],
        weight_sums[10],
    )


def solution(mesh):
    in_specs = (
        P("dp", None),
        P("dp", None),
        P("dp", None),
        P(),
        P(),
        P(),
        P(None, "tensor"),
        P(),
        P("dp", "tensor"),
        P("dp", "tensor"),
        P("dp", "tensor"),
        P("dp", "tensor"),
        P(),
        P("dp", "tensor"),
        P("dp", "tensor"),
        P("dp", "tensor"),
        P("dp", "tensor"),
        P(),
        P("dp", "tensor"),
        P("dp", "tensor"),
        P("dp", "tensor"),
    )
    out_specs = (
        P("dp", None),
        P("dp", None),
        P(("dp", "tensor"), None),
        P(None, "tensor"),
        P(),
        P("dp", "tensor"),
        P("dp", "tensor"),
        P("dp", "tensor"),
        P("dp", "tensor"),
        P(),
        P("dp", "tensor"),
        P("dp", "tensor"),
        P("dp", "tensor"),
        P("dp", "tensor"),
        P(),
        P("dp", "tensor"),
        P("dp", "tensor"),
        P("dp", "tensor"),
    )
    return jax.shard_map(
        on_device, mesh=mesh, in_specs=in_specs, out_specs=out_specs, check_vma=False
    )
```

profile of v0, /device:TPU:0, one launch (start us, length us, event | category | flops | bytes accessed | tf_op | source)
XLA Modules:
  0.0 1882.7 jit_solution(9294752748189345016)
XLA Ops:
  10.6 8.3 all-to-all-start.4
  19.7 15.5 all-to-all-done.4
  35.2 4.1 all-to-all-start
  40.1 16.1 all-to-all-done
  57.9 3.9 all-to-all-start.1
  62.3 215.5 %gather_fusion.1 = f32[65536,8]{1,0:T(8,128)} fusion(f32[8,256]{0,1:T(8,128)S(1)} %copy.116, s32[65536]{0:T(1024)S(1)} %broadcast_clamp_fusion), kind=kCustom, calls=%fused_computation.1.clone | custom fusion | bytes 4456448 | tf_op jit(solution)/shard_map/jit(_take)/gather | solution.py:109
  277.9 19.6 %copy.118 = f32[256,256,8]{0,1,2:T(8,128)} copy(f32[256,256,8]{2,1,0:T(8,128)} %bitcast.156) | data formatting | bytes 4194304 | tf_op jit(solution)/shard_map/jit(_take)/gather | solution.py:109
  312.5 2.6 convolution_convert_fusion.2
  315.9 7.0 all-to-all-start.5
  326.2 35.5 %all-gather.24.cloned.1.call-done = bf16[1024,512]{1,0:T(8,128)(2,1)} async-done(((bf16[64,512]{1,0:T(8,128)(2,1)}), bf16[1024,512]{1,0:T(8,128)(2,1)}) %all-gather.24.cloned.1.call-update) | async-done | bytes 1048592 | tf_op jit(solution)/shard_map/all_gather | solution.py:203
  364.2 18.0 all-reduce.9.cloned.1.call-done
  382.2 2.7 multiply_reduce_fusion.3
  384.9 56.9 %all-gather.22.cloned.1.call-done = bf16[1024,512]{1,0:T(8,128)(2,1)} async-done(((bf16[64,512]{1,0:T(8,128)(2,1)}), bf16[1024,512]{1,0:T(8,128)(2,1)}) %all-gather.22.cloned.1.call-update) | async-done | bytes 1048592 | tf_op jit(solution)/shard_map/all_gather | solution.py:202
  441.8 2.7 convolution_convert_fusion.14
  449.0 50.0 %all-gather.26.cloned.1.call-done = bf16[1024,512]{1,0:T(8,128)(2,1)} async-done(((bf16[64,512]{1,0:T(8,128)(2,1)}), bf16[1024,512]{1,0:T(8,128)(2,1)}) %all-gather.26.cloned.1.call-update) | async-done | bytes 1048592 | tf_op jit(solution)/shard_map/all_gather | solution.py:205
  499.1 2.5 convolution_convert_fusion.1
  503.9 15.6 all-reduce.11.cloned.1.call-done
  523.0 66.3 %all-gather.28.cloned.1.call-done = bf16[1024,1408]{1,0:T(8,128)(2,1)} async-done(((bf16[64,1408]{1,0:T(8,128)(2,1)}), bf16[1024,1408]{1,0:T(8,128)(2,1)}) %all-gather.28.cloned.1.call-update) | async-done | bytes 2883600 | tf_op jit(solution)/shard_map/all_gather | solution.py:206
  589.4 4.2 fusion.64
  593.5 63.4 %all-gather.30.cloned.1.call-done = bf16[1024,1408]{1,0:T(8,128)(2,1)} async-done(((bf16[64,1408]{1,0:T(8,128)(2,1)}), bf16[1024,1408]{1,0:T(8,128)(2,1)}) %all-gather.30.cloned.1.call-update) | async-done | bytes 2883600 | tf_op jit(solution)/shard_map/all_gather | solution.py:207
  657.0 4.1 fusion.65
  661.0 63.7 %all-gather.32.cloned.1.call-done = bf16[1024,1408]{1,0:T(8,128)(2,1)} async-done(((bf16[64,1408]{1,0:T(8,128)(2,1)}), bf16[1024,1408]{1,0:T(8,128)(2,1)}) %all-gather.32.cloned.1.call-update) | async-done | bytes 2883600 | tf_op jit(solution)/shard_map/all_gather | solution.py:208
  724.7 5.6 multiply_convert_fusion.2
  734.5 17.9 all-reduce.13.cloned.1.call-done
  765.6 3.9 convolution_convert_fusion.3
  769.5 15.9 all-reduce.15.cloned.1.call-done
  826.5 4.7 fusion.72
  831.5 4.6 fusion.73
  838.3 2.6 fusion.24
  840.9 25.1 %all_to_all.40 = bf16[16,16,1024]{2,1,0:T(8,128)(2,1)S(1)} all-to-all(bf16[16,16,1024]{2,1,0:T(8,128)(2,1)S(1)} %bitcast.186), channel_id=1, replica_groups=mesh['dp'=16,'tensor'=2] {'dp'}, dimensions={0} | all-to-all | bytes 1048576 | tf_op jit(solution)/shard_map/all_to_all | solution.py:370
  866.0 6.0 all-to-all-start.2
  872.7 17.1 all-to-all-done.2
  891.5 5.7 all-to-all-start.3
  897.3 4.6 fusion.74
  906.2 8.2 all-to-all-done.3
  914.4 4.4 all-to-all-start.7
  921.1 8.0 reshape.347
  929.1 2.6 reduce_sum.156
  932.0 77.2 %all-reduce.1 = (f32[32,8]{0,1:T(8,128)}, f32[1024]{0:T(1024)}, f32[1024]{0:T(1024)}, f32[1024]{0:T(1024)}) all-reduce(f32[32,8]{0,1:T(8,128)S(1)} %fusion.54, f32[1024]{0:T(1024)S(1)} %get-tuple-element.116, f32[1024]{0:T(1024)S(1)} %get-tuple-element.114, f32[1024]{0:T(1024)S(1)} %get-tuple-element.112), channel_id=1, replica_groups=mesh['dp'=16,'tensor'=2] {'dp'}, use_global_device_ids=true, to_apply=%region_22.25 | all-reduce | flops 3328 | bytes 26624 | tf_op jit(solution)/shard_map/psum | solution.py:361
  1009.2 74.9 %reduce-scatter.39.cloned.1.call-done = f32[64,512]{1,0:T(8,128)} async-done(((f32[1024,512]{1,0:T(8,128)}), f32[64,512]{1,0:T(8,128)}) %reduce-scatter.39.cloned.1.call-update) | async-done | bytes 131088
  1084.1 80.4 %reduce-scatter.29.cloned.1.call-done = f32[64,512]{1,0:T(8,128)} async-done(((f32[1024,512]{1,0:T(8,128)}), f32[64,512]{1,0:T(8,128)}) %reduce-scatter.29.cloned.1.call-update) | async-done | bytes 131088 | tf_op jit(solution)/shard_map/reduce_scatter | solution.py:320
  1164.5 80.7 %reduce-scatter.19.cloned.1.call-done = f32[64,512]{1,0:T(8,128)} async-done(((f32[1024,512]{1,0:T(8,128)}), f32[64,512]{1,0:T(8,128)}) %reduce-scatter.19.cloned.1.call-update) | async-done | bytes 131088 | tf_op jit(solution)/shard_map/reduce_scatter | solution.py:355
  1245.2 80.9 %reduce-scatter.21.cloned.1.call-done = f32[64,512]{1,0:T(8,128)} async-done(((f32[1024,512]{1,0:T(8,128)}), f32[64,512]{1,0:T(8,128)}) %reduce-scatter.21.cloned.1.call-update) | async-done | bytes 131088 | tf_op jit(solution)/shard_map/reduce_scatter | solution.py:356
  1326.1 80.8 %reduce-scatter.23.cloned.1.call-done = f32[64,512]{1,0:T(8,128)} async-done(((f32[1024,512]{1,0:T(8,128)}), f32[64,512]{1,0:T(8,128)}) %reduce-scatter.23.cloned.1.call-update) | async-done | bytes 131088 | tf_op jit(solution)/shard_map/reduce_scatter | solution.py:357
  1406.9 80.6 %reduce-scatter.25.cloned.1.call-done = f32[64,512]{1,0:T(8,128)} async-done(((f32[1024,512]{1,0:T(8,128)}), f32[64,512]{1,0:T(8,128)}) %reduce-scatter.25.cloned.1.call-update) | async-done | bytes 131088 | tf_op jit(solution)/shard_map/reduce_scatter | solution.py:358
  1487.4 125.7 %reduce-scatter.31.cloned.1.call-done = f32[64,1408]{1,0:T(8,128)} async-done(((f32[1024,1408]{1,0:T(8,128)}), f32[64,1408]{1,0:T(8,128)}) %reduce-scatter.31.cloned.1.call-update) | async-done | bytes 360464 | tf_op jit(solution)/shard_map/reduce_scatter | solution.py:321
  1613.1 129.7 %reduce-scatter.33.cloned.1.call-done = f32[64,1408]{1,0:T(8,128)} async-done(((f32[1024,1408]{1,0:T(8,128)}), f32[64,1408]{1,0:T(8,128)}) %reduce-scatter.33.cloned.1.call-update) | async-done | bytes 360464 | tf_op jit(solution)/shard_map/reduce_scatter | solution.py:322
  1742.9 129.9 %reduce-scatter.35.cloned.1.call-done = f32[64,1408]{1,0:T(8,128)} async-done(((f32[1024,1408]{1,0:T(8,128)}), f32[64,1408]{1,0:T(8,128)}) %reduce-scatter.35.cloned.1.call-update) | async-done | bytes 360464 | tf_op jit(solution)/shard_map/reduce_scatter | solution.py:323
  (309 shorter events, 110.8 us)
Async XLA Ops:
  7.2 316.5 %copy-start = (bf16[256,1024]{1,0:T(8,128)(2,1)S(1)}, bf16[256,1024]{1,0:T(8,128)(2,1)}, u32[]{:S(2)}) copy-start(bf16[256,1024]{1,0:T(8,128)(2,1)} %param.30) | copy-start | bytes 1572868
  7.2 32.2 %copy-start.65 = (s32[16]{0:T(128)S(1)}, s32[16]{0:T(128)}, u32[]{:S(2)}) copy-start(s32[16]{0:T(128)} %param.33) | copy-start | bytes 196
  7.2 294.5 %all-gather.12.cloned.1.call-start = ((), (), s32[]{:S(2)}) async-start(), calls=%async_computation.20 | async-start | bytes 1114112 | tf_op jit(solution)/shard_map/all_gather | solution.py:200
  7.9 296.3 %all-gather.14.cloned.1.call-start = ((), (), s32[]{:S(2)}) async-start(), calls=%async_computation.21 | async-start | bytes 1114112 | tf_op jit(solution)/shard_map/all_gather | solution.py:198
  8.7 297.4 %all-gather.16.cloned.1.call-start = ((), (), s32[]{:S(2)}) async-start(), calls=%async_computation.22 | async-start | bytes 1114112 | tf_op jit(solution)/shard_map/all_gather | solution.py:199
  9.4 303.1 %all-gather.18.cloned.1.call-start = ((), (), s32[]{:S(2)}) async-start(), calls=%async_computation.23 | async-start | bytes 1114112 | tf_op jit(solution)/shard_map/all_gather | solution.py:201
  10.0 313.7 %all-gather.20.cloned.1.call-start = ((), (), s32[]{:S(2)}) async-start(), calls=%async_computation.25 | async-start | bytes 1114112 | tf_op jit(solution)/shard_map/all_gather | solution.py:204
  10.6 24.6 %all-to-all-start.4 = ((bf16[16,16,1024]{2,1,0:T(8,128)(2,1)}), bf16[16,16,1024]{2,1,0:T(8,128)(2,1)S(1)}, u32[]{:S(2)}, u32[]{:S(2)}) async-start(bf16[16,16,1024]{2,1,0:T(8,128)(2,1)} %bitcast.197), calls=%async_computation.4 | async-start | bytes 1048576 | tf_op jit(solution)/shard_map/all_to_all | solution.py:179
  18.9 342.8 %all-gather.24.cloned.1.call-start = ((), (), s32[]{:S(2)}) async-start(), calls=%async_computation.27 | async-start | bytes 1114112 | tf_op jit(solution)/shard_map/all_gather | solution.py:203
  35.2 21.1 %all-to-all-start = ((bf16[16,16,1024]{2,1,0:T(8,128)(2,1)}), bf16[16,16,1024]{2,1,0:T(8,128)(2,1)S(1)}, u32[]{:S(2)}, u32[]{:S(2)}) async-start(bf16[16,16,1024]{2,1,0:T(8,128)(2,1)} %bitcast), calls=%async_computation | async-start | bytes 1048576 | tf_op jit(solution)/shard_map/all_to_all | solution.py:172
  40.1 21.8 %copy-start.67 = (f32[32,8]{0,1:T(8,128)S(1)}, f32[32,8]{0,1:T(8,128)}, u32[]{:S(2)}) copy-start(f32[32,8]{0,1:T(8,128)} %param.35) | copy-start | bytes 3076
  40.1 21.8 %copy-start.68 = (s32[256]{0:T(256)S(1)}, s32[256]{0:T(256)}, u32[]{:S(2)}) copy-start(s32[256]{0:T(256)} %param.34) | copy-start | bytes 3076
  57.9 243.1 %all-to-all-start.1 = ((bf16[16,16,1024]{2,1,0:T(8,128)(2,1)}), bf16[16,16,1024]{2,1,0:T(8,128)(2,1)S(1)}, u32[]{:S(2)}, u32[]{:S(2)}) async-start(bf16[16,16,1024]{2,1,0:T(8,128)(2,1)} %get-tuple-element.143), calls=%async_computation.1 | async-start | bytes 1048576 | tf_op jit(solution)/shard_map/all_to_all | solution.py:188
  61.9 320.3 %all-reduce.9.cloned.1.call-start = ((), (), s32[]{:S(2)}) async-start(), calls=%async_computation.24 | async-start | bytes 1048576 | tf_op jit(solution)/shard_map/psum | solution.py:130
  277.9 19.9 %copy-start.64 = (s32[16]{0:T(128)S(1)}, s32[16]{0:T(128)}, u32[]{:S(2)}) copy-start(s32[16]{0:T(128)} %param.32) | copy-start | bytes 196
  277.9 23.5 %copy-start.56 = (f32[1024]{0:T(1024)S(1)}, f32[1024]{0:T(1024)}, u32[]{:S(2)}) copy-start(f32[1024]{0:T(1024)} %param.36) | copy-start | bytes 12292
  315.1 126.7 %all-gather.22.cloned.1.call-start = ((), (), s32[]{:S(2)}) async-start(), calls=%async_computation.26 | async-start | bytes 1114112 | tf_op jit(solution)/shard_map/all_gather | solution.py:202
  315.9 48.3 %all-to-all-start.5 = ((bf16[16,16,1024]{2,1,0:T(8,128)(2,1)}), bf16[16,16,1024]{2,1,0:T(8,128)(2,1)}, u32[]{:S(2)}, u32[]{:S(2)}) async-start(bf16[16,16,1024]{2,1,0:T(8,128)(2,1)} %get-tuple-element.142), calls=%async_computation.5 | async-start | bytes 1048576 | tf_op jit(solution)/shard_map/all_to_all | solution.py:191
  322.9 176.2 %all-gather.26.cloned.1.call-start = ((), (), s32[]{:S(2)}) async-start(), calls=%async_computation.28 | async-start | bytes 1114112 | tf_op jit(solution)/shard_map/all_gather | solution.py:205
  323.6 58.6 %copy-start.60 = (f32[256]{0:T(256)S(1)}, f32[256]{0:T(256)}, u32[]{:S(2)}) copy-start(f32[256]{0:T(256)} %copy-done.59) | copy-start | bytes 3076
  323.6 195.9 %all-reduce.11.cloned.1.call-start = ((), (), s32[]{:S(2)}) async-start(), calls=%async_computation.29 | async-start | bytes 1048576 | tf_op jit(solution)/shard_map/psum | solution.py:130
  363.4 78.4 %copy-start.55 = (f32[1024]{0:T(1024)S(1)}, f32[1024]{0:T(1024)}, u32[]{:S(2)}) copy-start(f32[1024]{0:T(1024)} %param.41) | copy-start | bytes 12292
  449.0 72.1 %copy-start.49 = (bf16[8,64,256]{2,1,0:T(8,128)(2,1)}, bf16[8,64,256]{2,1,0:T(8,128)(2,1)S(1)}, u32[]{:S(2)}) copy-start(bf16[8,64,256]{2,1,0:T(8,128)(2,1)S(1)} %convolution_convert_fusion.12) | copy-start | bytes 786436
  501.6 20.5 %copy-start.58 = (f32[1024]{0:T(1024)S(1)}, f32[1024]{0:T(1024)}, u32[]{:S(2)}) copy-start(f32[1024]{0:T(1024)} %param.46) | copy-start | bytes 12292
  501.6 87.8 %all-gather.28.cloned.1.call-start = ((), (), s32[]{:S(2)}) async-start(), calls=%async_computation.30 | async-start | bytes 3063808 | tf_op jit(solution)/shard_map/all_gather | solution.py:206
  502.3 154.6 %all-gather.30.cloned.1.call-start = ((), (), s32[]{:S(2)}) async-start(), calls=%async_computation.31 | async-start | bytes 3063808 | tf_op jit(solution)/shard_map/all_gather | solution.py:207
  502.9 221.8 %all-gather.32.cloned.1.call-start = ((), (), s32[]{:S(2)}) async-start(), calls=%async_computation.32 | async-start | bytes 3063808 | tf_op jit(solution)/shard_map/all_gather | solution.py:208
  503.7 248.8 %all-reduce.13.cloned.1.call-start = ((), (), s32[]{:S(2)}) async-start(), calls=%async_computation.33 | async-start | bytes 1048576 | tf_op jit(solution)/shard_map/psum | solution.py:134
  734.5 50.9 %all-reduce.15.cloned.1.call-start = ((), (), s32[]{:S(2)}) async-start(), calls=%async_computation.34 | async-start | bytes 1048576 | tf_op jit(solution)/shard_map/psum | solution.py:134
  765.3 71.4 %all-reduce.17.cloned.1.call-start = ((), (), s32[]{:S(2)}) async-start(), calls=%async_computation.47 | async-start | bytes 2097152 | tf_op jit(solution)/shard_map/psum | solution.py:130
  800.3 208.9 %reduce-scatter.17.cloned.1.call-start = ((), (), s32[]{:S(2)}) async-start(), calls=%async_computation.35 | async-start | bytes 786432 | tf_op jit(solution)/shard_map/reduce_scatter | solution.py:308
  807.3 201.9 %reduce-scatter.27.cloned.1.call-start = ((), (), s32[]{:S(2)}) async-start(), calls=%async_computation.40 | async-start | bytes 2228224 | tf_op jit(solution)/shard_map/reduce_scatter | solution.py:317
  809.3 199.9 %reduce-scatter.37.cloned.1.call-start = ((), (), s32[]{:S(2)}) async-start(), calls=%async_computation.45 | async-start | bytes 2228224
  811.7 272.4 %reduce-scatter.39.cloned.1.call-start = ((), (), s32[]{:S(2)}) async-start(), calls=%async_computation.46 | async-start | bytes 2228224
  814.9 349.6 %reduce-scatter.29.cloned.1.call-start = ((), (), s32[]{:S(2)}) async-start(), calls=%async_computation.41 | async-start | bytes 2228224 | tf_op jit(solution)/shard_map/reduce_scatter | solution.py:320
  817.9 427.3 %reduce-scatter.19.cloned.1.call-start = ((), (), s32[]{:S(2)}) async-start(), calls=%async_computation.36 | async-start | bytes 2228224 | tf_op jit(solution)/shard_map/reduce_scatter | solution.py:355
  820.7 505.4 %reduce-scatter.21.cloned.1.call-start = ((), (), s32[]{:S(2)}) async-start(), calls=%async_computation.37 | async-start | bytes 2228224 | tf_op jit(solution)/shard_map/reduce_scatter | solution.py:356
  822.6 584.2 %reduce-scatter.23.cloned.1.call-start = ((), (), s32[]{:S(2)}) async-start(), calls=%async_computation.38 | async-start | bytes 2228224 | tf_op jit(solution)/shard_map/reduce_scatter | solution.py:357
  824.5 662.9 %reduce-scatter.25.cloned.1.call-start = ((), (), s32[]{:S(2)}) async-start(), calls=%async_computation.39 | async-start | bytes 2228224 | tf_op jit(solution)/shard_map/reduce_scatter | solution.py:358
  826.4 786.7 %reduce-scatter.31.cloned.1.call-start = ((), (), s32[]{:S(2)}) async-start(), calls=%async_computation.42 | async-start | bytes 6127616 | tf_op jit(solution)/shard_map/reduce_scatter | solution.py:321
  831.2 911.7 %reduce-scatter.33.cloned.1.call-start = ((), (), s32[]{:S(2)}) async-start(), calls=%async_computation.43 | async-start | bytes 6127616 | tf_op jit(solution)/shard_map/reduce_scatter | solution.py:322
  840.9 31.2 %copy-start.63 = (s32[16]{0:T(128)S(1)}, s32[16]{0:T(128)}, u32[]{:S(2)}) copy-start(s32[16]{0:T(128)} %get-tuple-element.140) | copy-start | bytes 196
  840.9 31.2 %copy-start.66 = (s32[16]{0:T(128)S(1)}, s32[16]{0:T(128)}, u32[]{:S(2)}) copy-start(s32[16]{0:T(128)} %param.33) | copy-start | bytes 196
  866.0 23.8 %all-to-all-start.2 = ((bf16[16,16,1024]{2,1,0:T(8,128)(2,1)}), bf16[16,16,1024]{2,1,0:T(8,128)(2,1)S(1)}, u32[]{:S(2)}, u32[]{:S(2)}) async-start(bf16[16,16,1024]{2,1,0:T(8,128)(2,1)} %bitcast.185), calls=%async_computation.2 | async-start | bytes 1048576 | tf_op jit(solution)/shard_map/all_to_all | solution.py:363
  872.7 24.6 %copy-start.24 = (bf16[256,1024]{1,0:T(8,128)(2,1)S(1)}, bf16[256,1024]{1,0:T(8,128)(2,1)}, u32[]{:S(2)}) copy-start(bf16[256,1024]{1,0:T(8,128)(2,1)} %get-tuple-element.137) | copy-start | bytes 1572868
  891.5 22.9 %all-to-all-start.3 = ((bf16[16,16,1024]{2,1,0:T(8,128)(2,1)}), bf16[16,16,1024]{2,1,0:T(8,128)(2,1)S(1)}, u32[]{:S(2)}, u32[]{:S(2)}) async-start(bf16[16,16,1024]{2,1,0:T(8,128)(2,1)} %get-tuple-element.139), calls=%async_computation.3 | async-start | bytes 1048576 | tf_op jit(solution)/shard_map/all_to_all | solution.py:379
  897.2 975.5 %reduce-scatter.35.cloned.1.call-start = ((), (), s32[]{:S(2)}) async-start(), calls=%async_computation.44 | async-start | bytes 6127616 | tf_op jit(solution)/shard_map/reduce_scatter | solution.py:323
  914.4 94.8 %all-to-all-start.7 = ((bf16[16,16,1024]{2,1,0:T(8,128)(2,1)}), bf16[16,16,1024]{2,1,0:T(8,128)(2,1)}, u32[]{:S(2)}, u32[]{:S(2)}) async-start(bf16[16,16,1024]{2,1,0:T(8,128)(2,1)} %get-tuple-element.138), calls=%async_computation.7 | async-start | bytes 1048576 | tf_op jit(solution)/shard_map/all_to_all | solution.py:386
  (57 other events, 121.8 us)
Sparse Core Ops, SparseCore 0:
  10.8 64.5 all-gather.11
  78.2 54.8 all-gather.13
  135.9 54.0 all-gather.15
  192.6 54.0 all-gather.17
  249.3 54.0 all-gather.19
  306.0 55.6 all-gather.23
  364.6 17.5 all-reduce.8
  385.3 56.4 all-gather.21
  444.9 54.0 all-gather.25
  501.9 17.5 all-reduce.10
  522.3 67.0 all-gather.27
  592.0 64.9 all-gather.29
  659.7 64.9 all-gather.31
  734.6 17.7 all-reduce.12
  765.4 19.9 all-reduce.14
  800.4 20.8 all-reduce.16
  824.1 9.1 reduce-scatter.16
  836.0 86.8 reduce-scatter.26
  925.7 77.9 reduce-scatter.36
  1006.4 77.6 reduce-scatter.38
  1087.0 77.5 reduce-scatter.28
  1167.4 77.8 reduce-scatter.18
  1248.1 77.9 reduce-scatter.20
  1328.8 78.0 reduce-scatter.22
  1409.7 77.6 reduce-scatter.24
  1490.2 122.9 reduce-scatter.30
  1615.9 126.9 reduce-scatter.32
  1745.7 126.9 reduce-scatter.34
where the time goes:
time: 1890 us; the launch traced here: 1880 us
  waiting for transfers between devices  1330 us (70%)
  local copies, waits for them, and re-layouts  278 us (15%)
  blocking collectives  102 us (5%)
  matrix products  84.3 us (4%)
  starting transfers between devices  41.3 us (2%)
  other arithmetic  29.4 us (2%)
    gather x2, local copies, waits for them, and re-layouts, self_block_scores(): raw_scores = raw_scores + jnp.take(distance_bias, distance, axis=1)  235 us
    reduce_scatter x1, waiting for transfers between devices, on_device(): lax.psum_scatter(down_weight_grad, 'dp', scatter_dimension=0, tiled=True)  130 us
    reduce_scatter x1, waiting for transfers between devices, on_device(): lax.psum_scatter(lift_weight_grad, 'dp', scatter_dimension=0, tiled=True)  130 us
    reduce_scatter x1, waiting for transfers between devices, on_device(): lax.psum_scatter(gate_weight_grad, 'dp', scatter_dimension=0, tiled=True)  126 us
    unnamed x30, waiting for transfers between devices  82.1 us
    reduce_scatter x1, waiting for transfers between devices, on_device(): lax.psum_scatter(key_weight_grad, 'dp', scatter_dimension=0, tiled=True)  80.9 us
    reduce_scatter x1, waiting for transfers between devices, on_device(): lax.psum_scatter(value_weight_grad, 'dp', scatter_dimension=0, tiled=True)  80.8 us
    reduce_scatter x1, waiting for transfers between devices, on_device(): lax.psum_scatter(query_weight_grad, 'dp', scatter_dimension=0, tiled=True)  80.7 us
  transfers between devices with their start and end apart: 35, of which 23 were waited for; matrix products, arithmetic and copies ran while one was open for 18% of the time, Pallas kernels for 0%

commit v1 on v0

v1 whole, which is shorter than its diff:
```python
import functools

import jax
import jax.numpy as jnp
import numpy as np
from jax import lax
from jax.experimental import pallas as pl
from jax.experimental.pallas import tpu as pltpu
from jax.sharding import PartitionSpec as P

EPSILON = 1e-06
MASKED = -1e30
HIGHEST = lax.Precision.HIGHEST
HEAD = 64
PAIR = 2 * HEAD


def exchange_masks(devices):
    width = devices.bit_length() - 1
    upper = [1 << bit for bit in range(width - 1, 1, -1)]
    if devices == 16:
        upper = [12, 4]
    lower = [mask for mask in (1, 2) if mask < devices]
    return {
        "a": upper + lower,
        "b": upper + lower[::-1],
        "z": lower + upper,
    }


def block_offsets(masks):
    offsets = [0]
    for mask in masks:
        offsets = offsets + [offset ^ mask for offset in offsets]
    return offsets


def swap_dp(value, mask, devices):
    return lax.ppermute(value, "dp", [(one, one ^ mask) for one in range(devices)])


def swap_tensor(value):
    return lax.ppermute(value, "tensor", [(0, 1), (1, 0)])


def reorder_blocks(value, from_masks, to_masks):
    before = block_offsets(from_masks)
    after = block_offsets(to_masks)
    rows = value.shape[0] // len(before)
    places = [before.index(offset) for offset in after]
    runs = []
    for place in places:
        if runs and runs[-1][1] == place:
            runs[-1][1] = place + 1
        else:
            runs.append([place, place + 1])
    if len(runs) == 1:
        return value
    return jnp.concatenate(
        [value[first * rows : last * rows] for first, last in runs], axis=0
    )


def gather_rows(value, masks, devices):
    for mask in masks:
        value = jnp.concatenate([value, swap_dp(value, mask, devices)], axis=0)
    return value


def reduce_rows(value, masks, devices):
    for mask in masks[::-1]:
        half = value.shape[0] // 2
        away = value[half:].astype(jnp.bfloat16)
        value = value[:half].astype(jnp.float32) + swap_dp(away, mask, devices).astype(
            jnp.float32
        )
    return value


def total_small(value, devices):
    mask = 1
    while mask < devices:
        value = value + swap_dp(value, mask, devices)
        mask = 2 * mask
    return value


def product_plain(left, right):
    return jnp.dot(left, right, preferred_element_type=jnp.float32)


def product_right(left, right):
    return lax.dot_general(
        left, right, (((1,), (1,)), ((), ())), preferred_element_type=jnp.float32
    )


def product_left(left, right):
    return lax.dot_general(
        left, right, (((0,), (0,)), ((), ())), preferred_element_type=jnp.float32
    )


def norm_forward(activation, gain_in):
    inv_root = lax.rsqrt(jnp.mean(activation * activation, axis=-1, keepdims=True) + EPSILON)
    return (activation * inv_root * gain_in, inv_root)


def norm_backward(activation, inv_root, gain_in, upstream):
    weighted = upstream * gain_in
    inner_mean = jnp.mean(weighted * activation, axis=-1, keepdims=True)
    grad_in = inv_root * weighted - activation * (inv_root * inv_root * inv_root) * inner_mean
    return (grad_in, jnp.sum(upstream * activation * inv_root, axis=0))


def toeplitz_bias(row, rows):
    wide = jnp.broadcast_to(row, (rows, row.shape[1]))
    return pltpu.roll(wide, 0, 1, stride=1, stride_axis=0)[:, :rows]


def head_half(value, side, lanes):
    keep = lanes < HEAD if side == 0 else lanes >= HEAD
    return jnp.where(keep, value, jnp.zeros_like(value))


def masked_scores(query, key, length_ref, bias_ref, head):
    scores = product_right(query, key)
    if bias_ref is None:
        return scores
    rows, columns = scores.shape
    scores = scores + toeplitz_bias(bias_ref[pl.ds(head, 1), :], rows)
    at_row = lax.broadcasted_iota(jnp.int32, (rows, columns), 0)
    at_column = lax.broadcasted_iota(jnp.int32, (rows, columns), 1)
    allowed = (at_column <= at_row) & (at_column < length_ref[0])
    return jnp.where(allowed, scores, MASKED)


def softmax_rows(scores):
    exponent = jnp.exp(scores - jnp.max(scores, axis=-1, keepdims=True))
    return exponent / jnp.sum(exponent, axis=-1, keepdims=True)


def attention_forward_body(biased, *refs):
    if biased:
        length_ref, bias_ref, query_ref, key_ref, value_ref, out_ref = refs
    else:
        query_ref, key_ref, value_ref, out_ref = refs
        length_ref = bias_ref = None
    rows, width = query_ref.shape
    lanes = lax.broadcasted_iota(jnp.int32, (rows, PAIR), 1)

    def one_pair(pair, carry):
        columns = pl.ds(pl.multiple_of(pair * PAIR, PAIR), PAIR)
        query, key, value = query_ref[:, columns], key_ref[:, columns], value_ref[:, columns]
        mixed = []
        for side in range(2):
            scores = masked_scores(
                head_half(query, side, lanes), key, length_ref, bias_ref, 2 * pair + side
            )
            chance = softmax_rows(scores).astype(jnp.bfloat16)
            mixed.append(product_plain(chance, value))
        out_ref[:, columns] = jnp.where(lanes < HEAD, mixed[0], mixed[1]).astype(jnp.bfloat16)
        return carry

    lax.fori_loop(0, width // PAIR, one_pair, 0)


def attention_backward_body(biased, *refs):
    if biased:
        (
            length_ref,
            bias_ref,
            query_ref,
            key_ref,
            value_ref,
            grad_ref,
            dquery_ref,
            dkey_ref,
            dvalue_ref,
            diagonal_ref,
        ) = refs
    else:
        query_ref, key_ref, value_ref, grad_ref, dquery_ref, dkey_ref, dvalue_ref = refs
        length_ref = bias_ref = diagonal_ref = None
    rows, width = query_ref.shape
    lanes = lax.broadcasted_iota(jnp.int32, (rows, PAIR), 1)
    if biased:
        flip = (
            lax.broadcasted_iota(jnp.int32, (rows, rows), 0)
            + lax.broadcasted_iota(jnp.int32, (rows, rows), 1)
            == rows - 1
        ).astype(jnp.bfloat16)

    def one_pair(pair, carry):
        columns = pl.ds(pl.multiple_of(pair * PAIR, PAIR), PAIR)
        query, key, value = query_ref[:, columns], key_ref[:, columns], value_ref[:, columns]
        grad = grad_ref[:, columns]
        dquery, dkey, dvalue = [], [], []
        for side in range(2):
            head = 2 * pair + side
            scores = masked_scores(
                head_half(query, side, lanes), key, length_ref, bias_ref, head
            )
            chance = softmax_rows(scores)
            chance_grad = product_right(head_half(grad, side, lanes), value)
            delta = jnp.sum(chance * chance_grad, axis=-1, keepdims=True)
            score_grad = (chance * (chance_grad - delta)).astype(jnp.bfloat16)
            dquery.append(product_plain(score_grad, key))
            dkey.append(product_left(score_grad, query))
            dvalue.append(product_left(chance.astype(jnp.bfloat16), grad))
            if biased:
                flipped = product_plain(flip, score_grad)
                wide = jnp.concatenate([flipped, jnp.zeros_like(flipped)], axis=1)
                skewed = pltpu.roll(wide, rows + 1, 1, stride=1, stride_axis=0)
                diagonal_ref[pl.ds(head, 1), :] = jnp.sum(skewed, axis=0, keepdims=True)
        left = lanes < HEAD
        dquery_ref[:, columns] = jnp.where(left, dquery[0], dquery[1]).astype(jnp.bfloat16)
        dkey_ref[:, columns] = jnp.where(left, dkey[0], dkey[1]).astype(jnp.bfloat16)
        dvalue_ref[:, columns] = jnp.where(left, dvalue[0], dvalue[1]).astype(jnp.bfloat16)
        return carry

    lax.fori_loop(0, width // PAIR, one_pair, 0)


def vmem():
    return pl.BlockSpec(memory_space=pltpu.VMEM)


def smem():
    return pl.BlockSpec(memory_space=pltpu.SMEM)


def attention_forward(query, key, value, length=None, bias=None):
    biased = bias is not None
    extra = (length, bias) if biased else ()
    specs = [smem(), vmem()] if biased else []
    return pl.pallas_call(
        functools.partial(attention_forward_body, biased),
        out_shape=jax.ShapeDtypeStruct(query.shape, jnp.bfloat16),
        in_specs=specs + [vmem()] * 3,
        out_specs=vmem(),
        compiler_params=pltpu.CompilerParams(vmem_limit_bytes=32 << 20),
    )(*extra, query, key, value)


def attention_backward(query, key, value, grad, length=None, bias=None):
    biased = bias is not None
    extra = (length, bias) if biased else ()
    specs = [smem(), vmem()] if biased else []
    out_shape = [jax.ShapeDtypeStruct(query.shape, jnp.bfloat16)] * 3
    if biased:
        out_shape = out_shape + [jax.ShapeDtypeStruct(bias.shape, jnp.float32)]
    return pl.pallas_call(
        functools.partial(attention_backward_body, biased),
        out_shape=out_shape,
        in_specs=specs + [vmem()] * 4,
        out_specs=[vmem()] * len(out_shape),
        compiler_params=pltpu.CompilerParams(vmem_limit_bytes=32 << 20),
    )(*extra, query, key, value, grad)


def gelu_product(gate_pre, lift_pre):
    return jax.nn.gelu(gate_pre, approximate=True) * lift_pre


def pair_total(partial_value):
    mine = partial_value.astype(jnp.bfloat16)
    return mine.astype(jnp.float32) + swap_tensor(mine).astype(jnp.float32)


def deal(value, order, devices):
    rows, width = value.shape
    first = lax.all_to_all(
        value.reshape(devices, rows // devices, width), "dp", split_axis=0, concat_axis=0, tiled=True
    )
    second = lax.all_to_all(
        jnp.take(first, order, axis=0), "dp", split_axis=0, concat_axis=0, tiled=True
    )
    return second.reshape(rows, width)


def on_device(
    tokens,
    encoder_states,
    cotangent,
    lengths,
    deal_order,
    bucket_index,
    rel_table,
    gain_self,
    self_query,
    self_key,
    self_value,
    self_output,
    gain_cross,
    cross_query,
    cross_key,
    cross_value,
    cross_output,
    gain_feed,
    feed_gate,
    feed_value,
    feed_output,
):
    devices = lax.axis_size("dp")
    myself = lax.axis_index("dp")
    core = lax.axis_index("tensor")
    length_all, model_width = tokens.shape
    block = model_width // devices
    buckets, head_count = rel_table.shape
    inner = self_query.shape[1]
    feed = feed_gate.shape[1]
    masks = exchange_masks(devices)
    order_a, order_b, order_z = masks["a"], masks["b"], masks["z"]

    numbers = jnp.arange(devices, dtype=jnp.int32)
    owner_of = jnp.sum(
        jnp.where(deal_order[:, None] == numbers[None, :], numbers[:, None], 0), axis=0
    )
    my_length = jnp.sum(jnp.where(numbers == myself, lengths, 0))
    length_ref = my_length.reshape(1)

    def gathered(parts, order):
        whole = gather_rows(jnp.concatenate(parts, axis=1), order, devices)
        return reorder_blocks(whole, order, order_a)

    low_qk = gathered((self_query, self_key), order_a)
    low_vo = gathered((self_value, self_output), order_b)
    cross_kv = gathered((cross_key, cross_value), order_a)
    cross_qo = gathered((cross_query, cross_output), order_b)
    gate_weight = gathered((feed_gate,), order_a)
    lift_weight = gathered((feed_value,), order_b)
    down_weight = gathered((feed_output,), order_z)
    query_weight, key_weight = low_qk[:, :inner], low_qk[:, inner:]
    value_weight, output_weight = low_vo[:, :inner], low_vo[:, inner:]
    cross_key_weight, cross_value_weight = cross_kv[:, :inner], cross_kv[:, inner:]
    cross_query_weight, cross_output_weight = cross_qo[:, :inner], cross_qo[:, inner:]

    offsets = jnp.asarray(np.array(block_offsets(order_a), np.int32))
    source_column = (
        ((myself ^ offsets) * block)[:, None] + jnp.arange(block, dtype=jnp.int32)[None, :]
    ).reshape(-1)
    columns = jnp.arange(model_width, dtype=jnp.int32)
    permute = (columns[:, None] == source_column[None, :]).astype(jnp.bfloat16)
    gains = jnp.dot(
        jnp.stack([gain_self, gain_cross, gain_feed]), permute.astype(jnp.float32), precision=HIGHEST
    )
    gain_self, gain_cross, gain_feed = gains[0], gains[1], gains[2]

    half = length_all // 2
    memory_half = deal(
        lax.dynamic_slice_in_dim(encoder_states, core * half, half, axis=0), deal_order, devices
    )
    memory = jnp.concatenate([memory_half, swap_tensor(memory_half)], axis=0)
    memory = product_plain(memory, permute).astype(jnp.bfloat16)

    positions = jnp.arange(length_all, dtype=jnp.int32)
    valid_rows = (positions < my_length).astype(jnp.float32)[:, None]
    skewed_bucket = jnp.concatenate(
        [
            bucket_index[:1],
            jnp.full((length_all,), -1, jnp.int32),
            bucket_index[::-1][: length_all - 1],
        ]
    )
    onehot_bucket = (
        jnp.arange(buckets, dtype=jnp.int32)[:, None] == skewed_bucket[None, :]
    ).astype(jnp.float32)
    bias_rows = jnp.dot(rel_table.T, onehot_bucket, precision=HIGHEST)

    masked_input = product_plain(tokens, permute) * valid_rows
    grad_three = product_plain(cotangent, permute) * valid_rows

    normed_self, root_self = norm_forward(masked_input, gain_self)
    normed_self_low = normed_self.astype(jnp.bfloat16)
    query_self = product_plain(normed_self_low, query_weight).astype(jnp.bfloat16)
    key_self = product_plain(normed_self_low, key_weight).astype(jnp.bfloat16)
    value_self = product_plain(normed_self_low, value_weight).astype(jnp.bfloat16)
    self_mixed_low = attention_forward(query_self, key_self, value_self, length_ref, bias_rows)
    hidden_one = masked_input + pair_total(product_right(self_mixed_low, output_weight))
    normed_cross, root_cross = norm_forward(hidden_one, gain_cross)
    normed_cross_low = normed_cross.astype(jnp.bfloat16)
    query_cross = product_plain(normed_cross_low, cross_query_weight).astype(jnp.bfloat16)
    key_cross = product_plain(memory, cross_key_weight).astype(jnp.bfloat16)
    value_cross = product_plain(memory, cross_value_weight).astype(jnp.bfloat16)
    cross_mixed_low = attention_forward(query_cross, key_cross, value_cross)
    hidden_two = hidden_one + pair_total(product_right(cross_mixed_low, cross_output_weight))
    normed_feed, root_feed = norm_forward(hidden_two, gain_feed)
    normed_feed_low = normed_feed.astype(jnp.bfloat16)
    gate_pre = product_plain(normed_feed_low, gate_weight)
    lift_pre = product_plain(normed_feed_low, lift_weight)
    hidden_low = gelu_product(gate_pre, lift_pre).astype(jnp.bfloat16)
    hidden_three = hidden_two + pair_total(product_right(hidden_low, down_weight))
    layer_result = (hidden_three * valid_rows).astype(jnp.bfloat16)
    layer_result = product_right(layer_result, permute).astype(jnp.bfloat16)

    def summed(grad, order):
        return reduce_rows(
            reorder_blocks(grad.astype(jnp.bfloat16), order_a, order), order, devices
        )

    branch_grad = grad_three.astype(jnp.bfloat16)
    hidden_grad = product_plain(branch_grad, down_weight).astype(jnp.bfloat16)
    gate_grad, lift_grad = jax.vjp(gelu_product, gate_pre, lift_pre)[1](
        hidden_grad.astype(jnp.float32)
    )
    gate_grad_low = gate_grad.astype(jnp.bfloat16)
    lift_grad_low = lift_grad.astype(jnp.bfloat16)
    down_sum = summed(product_left(branch_grad, hidden_low), order_z)
    gate_sum = summed(product_left(normed_feed_low, gate_grad_low), order_a)
    lift_sum = summed(product_left(normed_feed_low, lift_grad_low), order_b)
    feed_normed_grad = pair_total(
        product_right(gate_grad_low, gate_weight) + product_right(lift_grad_low, lift_weight)
    )
    back_feed, gain_feed_grad = norm_backward(hidden_two, root_feed, gain_feed, feed_normed_grad)
    grad_two = grad_three + back_feed
    branch_grad = grad_two.astype(jnp.bfloat16)
    mixed_grad = product_plain(branch_grad, cross_output_weight).astype(jnp.bfloat16)
    query_grad_low, key_grad_low, value_grad_low = attention_backward(
        query_cross, key_cross, value_cross, mixed_grad
    )
    kv_sum = summed(
        product_left(memory, jnp.concatenate([key_grad_low, value_grad_low], axis=1)), order_a
    )
    qo_sum = summed(
        jnp.concatenate(
            [
                product_left(normed_cross_low, query_grad_low),
                product_left(branch_grad, cross_mixed_low),
            ],
            axis=1,
        ),
        order_b,
    )
    encoder_partial = (
        product_right(key_grad_low, cross_key_weight)
        + product_right(value_grad_low, cross_value_weight)
    ).astype(jnp.bfloat16)
    encoder_half = (
        encoder_partial[:half].astype(jnp.float32)
        + swap_tensor(encoder_partial[half:]).astype(jnp.float32)
    ).astype(jnp.bfloat16)
    encoder_half = product_right(encoder_half, permute).astype(jnp.bfloat16)
    encoder_grad = deal(encoder_half, owner_of, devices)
    cross_normed_grad = pair_total(product_right(query_grad_low, cross_query_weight))
    back_cross, gain_cross_grad = norm_backward(
        hidden_one, root_cross, gain_cross, cross_normed_grad
    )
    grad_one = grad_two + back_cross
    branch_grad = grad_one.astype(jnp.bfloat16)
    mixed_grad = product_plain(branch_grad, output_weight).astype(jnp.bfloat16)
    query_grad_low, key_grad_low, value_grad_low, diagonal = attention_backward(
        query_self, key_self, value_self, mixed_grad, length_ref, bias_rows
    )
    table_grad = lax.dot_general(
        onehot_bucket, diagonal, (((1,), (1,)), ((), ())), precision=HIGHEST
    )
    low_qk_sum = summed(
        product_left(normed_self_low, jnp.concatenate([query_grad_low, key_grad_low], axis=1)),
        order_a,
    )
    low_vo_sum = summed(
        jnp.concatenate(
            [
                product_left(normed_self_low, value_grad_low),
                product_left(branch_grad, self_mixed_low),
            ],
            axis=1,
        ),
        order_b,
    )
    self_normed_grad = pair_total(
        product_right(query_grad_low, query_weight)
        + product_right(key_grad_low, key_weight)
        + product_right(value_grad_low, value_weight)
    )
    back_self, gain_self_grad = norm_backward(masked_input, root_self, gain_self, self_normed_grad)
    input_grad = ((grad_one + back_self) * valid_rows).astype(jnp.bfloat16)
    input_grad = product_right(input_grad, permute).astype(jnp.bfloat16)

    gain_grads = lax.dot_general(
        jnp.stack([gain_self_grad, gain_cross_grad, gain_feed_grad]),
        permute.astype(jnp.float32),
        (((1,), (1,)), ((), ())),
        precision=HIGHEST,
    )
    small = total_small(
        jnp.concatenate([gain_grads.reshape(-1), table_grad.reshape(-1)]).reshape(-1, 128), devices
    ).reshape(-1)
    gain_sums = small[: 3 * model_width].reshape(3, model_width)
    table_sum = small[3 * model_width :].reshape(buckets, head_count)
    return (
        layer_result,
        input_grad,
        encoder_grad,
        table_sum,
        gain_sums[0],
        low_qk_sum[:, :inner],
        low_qk_sum[:, inner:],
        low_vo_sum[:, :inner],
        low_vo_sum[:, inner:],
        gain_sums[1],
        qo_sum[:, :inner],
        kv_sum[:, :inner],
        kv_sum[:, inner:],
        qo_sum[:, inner:],
        gain_sums[2],
        gate_sum,
        lift_sum,
        down_sum,
    )


def solution(mesh):
    in_specs = (
        P("dp", None),
        P("dp", None),
        P("dp", None),
        P(),
        P(),
        P(),
        P(None, "tensor"),
        P(),
        P("dp", "tensor"),
        P("dp", "tensor"),
        P("dp", "tensor"),
        P("dp", "tensor"),
        P(),
        P("dp", "tensor"),
        P("dp", "tensor"),
        P("dp", "tensor"),
        P("dp", "tensor"),
        P(),
        P("dp", "tensor"),
        P("dp", "tensor"),
        P("dp", "tensor"),
    )
    out_specs = (
        P("dp", None),
        P("dp", None),
        P(("dp", "tensor"), None),
        P(None, "tensor"),
        P(),
        P("dp", "tensor"),
        P("dp", "tensor"),
        P("dp", "tensor"),
        P("dp", "tensor"),
        P(),
        P("dp", "tensor"),
        P("dp", "tensor"),
        P("dp", "tensor"),
        P("dp", "tensor"),
        P(),
        P("dp", "tensor"),
        P("dp", "tensor"),
        P("dp", "tensor"),
    )
    return jax.shard_map(
        on_device, mesh=mesh, in_specs=in_specs, out_specs=out_specs, check_vma=False
    )
```

time: 1890 us -> 456 us (0.24)
  waiting for transfers between devices: 1330 us -> 103 us
  local copies, waits for them, and re-layouts: 278 us -> 85.4 us
  blocking collectives: 102 us -> 0 us
  starting transfers between devices: 41.3 us -> 109 us
  other arithmetic: 29.4 us -> 67.3 us
  matrix products: 84.3 us -> 60.2 us
  Pallas kernels: 0 us -> 20.5 us
    reduce_scatter x10 -> x0, waiting for transfers between devices: 789 us -> none  [the longest x1 130 us: on_device(): lax.psum_scatter(down_weight_grad, 'dp', scatter_dimension=0, tiled=True)]
    all_gather x11 -> x0, waiting for transfers between devices: 336 us -> none  [the longest x1 66.3 us: on_device(): lax.all_gather(feed_gate, 'dp', axis=0, tiled=True)]
    gather x6 -> x2, local copies, waits for them, and re-layouts: 238 us -> 2.78 us  [deal(): jnp.take(first, order, axis=0)]
    ppermute x0 -> x68, waiting for transfers between devices: none -> 103 us  [the longest x60 103 us: swap_dp(): lax.ppermute(value, 'dp', [(one, one ^ mask) for one in range(devices)])]
    ppermute x0 -> x68, starting transfers between devices: none -> 87.5 us  [the longest x60 86.2 us: swap_dp(): lax.ppermute(value, 'dp', [(one, one ^ mask) for one in range(devices)])]
    unnamed x30 -> x0, waiting for transfers between devices: 82.1 us -> none
    psum x1 -> x0, blocking collectives: 77.2 us -> none  [on_device(): lax.psum((table_grad, gain_self_grad, gain_cross_grad, gain_feed_grad), '...]
    psum x5 -> x0, waiting for transfers between devices: 67.4 us -> none  [the longest x2 33.8 us: input_total(): lax.psum(partial_value.astype(jnp.bfloat16), 'tensor').astype(jnp.float32)]
  transfers between devices with their start and end apart: 35 -> 72, of which waited for: 23 -> 22; matrix products, arithmetic and copies ran while one was open for 18% -> 42% of each run, Pallas kernels for 0% -> 5%
where the time goes in v1:
time: 456 us; the launch traced here: 448 us
  starting transfers between devices  109 us (24%)
  waiting for transfers between devices  103 us (23%)
  local copies, waits for them, and re-layouts  85.4 us (19%)
  other arithmetic  67.3 us (15%)
  matrix products  60.2 us (13%)
  Pallas kernels  20.5 us (4%)
    ppermute x60, waiting for transfers between devices, swap_dp(): lax.ppermute(value, 'dp', [(one, one ^ mask) for one in range(devices)])  103 us
    ppermute x60, starting transfers between devices, swap_dp(): lax.ppermute(value, 'dp', [(one, one ^ mask) for one in range(devices)])  86.2 us
    unnamed x239, local copies, waits for them, and re-layouts  50.9 us
    dot_general x14, matrix products, product_right(): lax.dot_general(left, right, (((1,), (1,)), ((), ())), preferred_element_...  27.4 us
    concatenate x21, other arithmetic, gather_rows(): value = jnp.concatenate([value, swap_dp(value, mask, devices)], axis=0)  25 us
    add x28, other arithmetic, reduce_rows(): value[:half].astype(jnp.float32)  22.9 us
    dot_general x14, matrix products, product_plain(): return jnp.dot(left, right, preferred_element_type=jnp.float32)  21.4 us
    slice x24, local copies, waits for them, and re-layouts, reduce_rows(): away = value[half:].astype(jnp.bfloat16)  14.4 us
  transfers between devices with their start and end apart: 72, of which 22 were waited for; matrix products, arithmetic and copies ran while one was open for 42% of the time, Pallas kernels for 5%

profile of v1, /device:TPU:0, one launch (start us, length us, event | category | flops | bytes accessed | tf_op | source)
XLA Modules:
  0.0 448.5 jit_solution(17762903130746862050)
XLA Ops:
  0.8 5.1 %collective-permute-start.19 = (bf16[64,1408]{1,0:T(8,128)(2,1)}, bf16[64,1408]{1,0:T(8,128)(2,1)S(1)}, u32[]{:S(2)}, u32[]{:S(2)}) collective-permute-start(bf16[64,1408]{1,0:T(8,128)(2,1)} %param.42), channel_id=1, source_target_pairs={{0,24},{2,26},{4,28},{6,30},{8,16},{10,18},{12,20},{14,22},{16,8},... | collective-permute-start | bytes 540680 | tf_op jit(solution)/shard_map/ppermute | solution.py:39
  9.3 6.0 %all-to-all-start = ((bf16[16,8,1024]{2,1,0:T(8,128)(2,1)}), bf16[16,8,1024]{2,1,0:T(8,128)(2,1)}, u32[]{:S(2)}, u32[]{:S(2)}) async-start(bf16[16,8,1024]{2,1,0:T(8,128)(2,1)} %dynamic-slice_bitcast_fusion), calls=%async_computation | async-start | bytes 524288 | tf_op jit(solution)/shard_map/all_to_all | solution.py:273
  18.3 3.7 collective-permute-start
  42.6 3.7 collective-permute-start.9
  50.0 2.7 collective-permute-start.1
  53.4 2.8 collective-permute-done.14
  56.9 2.1 collective-permute-start.10
  60.5 2.1 collective-permute-start.20
  81.7 2.2 gather_fusion
  85.7 5.5 %all-to-all-start.1 = ((bf16[16,8,1024]{2,1,0:T(8,128)(2,1)}), bf16[16,8,1024]{2,1,0:T(8,128)(2,1)}, u32[]{:S(2)}, u32[]{:S(2)}) async-start(bf16[16,8,1024]{2,1,0:T(8,128)(2,1)} %broadcast_select_fusion.1), calls=%async_computation.1 | async-start | bytes 524288 | tf_op jit(solution)/shard_map/all_to_all | solution.py:276
  91.2 2.1 collective-permute-start.11
  102.5 2.1 pad_maximum_fusion.4
  104.6 3.8 collective-permute-start.29
  108.5 2.1 pad_maximum_fusion.5
  132.0 10.5 %collective-permute-done.3 = bf16[512,1024]{1,0:T(8,128)(2,1)S(1)} collective-permute-done((bf16[512,1024]{1,0:T(8,128)(2,1)}, bf16[512,1024]{1,0:T(8,128)(2,1)S(1)}, u32[]{:S(2)}, u32[]{:S(2)}) %collective-permute-start.3) | collective-permute-done | bytes 1048608 | tf_op jit(solution)/shard_map/ppermute | solution.py:39
  154.0 4.7 %shard_map.349 = bf16[256,512]{1,0:T(8,128)(2,1)S(1)} custom-call(s32[1]{0:T(128)} %bitcast.1.refs_0_, f32[8,512]{1,0:T(8,128)S(1)} %convolution_bitcast_fusion.refs_1_, bf16[256,512]{1,0:T(8,128)(2,1)S(1)} %convolution_convert_fusion.21.refs_2_, bf16[256,512]{1,0:T(8,128)(2,1)S(1)} %convolution_convert_fusion.20.refs_3_, ...), custom_call_target="tpu_custom_call" | custom-call | tf_op jit(solution)/shard_map/pallas_call | solution.py:237
  160.4 4.6 %collective-permute-done.17 = bf16[512,1024]{1,0:T(8,128)(2,1)S(1)} collective-permute-done((bf16[512,1024]{1,0:T(8,128)(2,1)S(1)}, bf16[512,1024]{1,0:T(8,128)(2,1)S(1)}, u32[]{:S(2)}, u32[]{:S(2)}) %collective-permute-start.17) | collective-permute-done | bytes 1048608 | tf_op jit(solution)/shard_map/ppermute | solution.py:39
  170.3 3.8 shard_map.350
  174.7 4.5 %collective-permute-done.30 = bf16[512,1408]{1,0:T(8,128)(2,1)S(1)} collective-permute-done((bf16[512,1408]{1,0:T(8,128)(2,1)S(1)}, bf16[512,1408]{1,0:T(8,128)(2,1)S(1)}, u32[]{:S(2)}, u32[]{:S(2)}) %collective-permute-start.30) | collective-permute-done | bytes 1441824 | tf_op jit(solution)/shard_map/ppermute | solution.py:39
  182.3 13.1 %collective-permute-done.22 = bf16[512,1408]{1,0:T(8,128)(2,1)S(1)} collective-permute-done((bf16[512,1408]{1,0:T(8,128)(2,1)S(1)}, bf16[512,1408]{1,0:T(8,128)(2,1)S(1)}, u32[]{:S(2)}, u32[]{:S(2)}) %collective-permute-start.22) | collective-permute-done | bytes 1441824 | tf_op jit(solution)/shard_map/ppermute | solution.py:39
  202.1 2.8 fusion.132
  205.0 3.9 fusion.30
  210.8 2.8 fusion.133
  215.7 3.9 fusion.44
  234.1 5.3 %shard_map.351 = (bf16[256,512]{1,0:T(8,128)(2,1)S(1)}, bf16[256,512]{1,0:T(8,128)(2,1)S(1)}, bf16[256,512]{1,0:T(8,128)(2,1)S(1)}) custom-call(bf16[256,512]{1,0:T(8,128)(2,1)S(1)} %convolution_convert_fusion.18.refs_0_, bf16[256,512]{1,0:T(8,128)(2,1)S(1)} %convolution_convert_fusion.17.refs_1_, bf16[256,512]{1,0:T(8,128)(2,1)S(1)} %convolution_convert_fusion.16.refs_2_, ...), custom_call_target="tpu_custom_call" | custom-call | tf_op jit(solution)/shard_map/pallas_call | solution.py:253
  251.9 4.2 all-to-all-start.2
  261.3 2.1 convolution_convert_fusion.14.refs_5_
  263.9 6.6 %shard_map.352 = (bf16[256,512]{1,0:T(8,128)(2,1)S(1)}, bf16[256,512]{1,0:T(8,128)(2,1)S(1)}, bf16[256,512]{1,0:T(8,128)(2,1)S(1)}, f32[8,512]{1,0:T(8,128)S(1)}) custom-call(s32[1]{0:T(128)} %bitcast.1.refs_0_, f32[8,512]{1,0:T(8,128)S(1)} %convolution_bitcast_fusion.refs_1_, bf16[256,512]{1,0:T(8,128)(2,1)S(1)} %convolution_convert_fusion.21.refs_2_, ...), custom_call_target="tpu_custom_call" | custom-call | tf_op jit(solution)/shard_map/pallas_call | solution.py:253
  270.5 2.7 fusion.70
  273.8 2.7 fusion.73
  276.5 2.1 convolution_convert_fusion.5
  279.8 2.3 slice.582
  284.0 2.7 fusion.45
  288.1 5.8 %all-to-all-start.3 = ((bf16[16,8,1024]{2,1,0:T(8,128)(2,1)}), bf16[16,8,1024]{2,1,0:T(8,128)(2,1)S(1)}, u32[]{:S(2)}, u32[]{:S(2)}) async-start(bf16[16,8,1024]{2,1,0:T(8,128)(2,1)} %broadcast_select_fusion), calls=%async_computation.3 | async-start | bytes 524288 | tf_op jit(solution)/shard_map/all_to_all | solution.py:276
  313.0 15.8 %collective-permute-done.36 = f32[26,128]{1,0:T(8,128)S(1)} collective-permute-done((f32[26,128]{1,0:T(8,128)S(1)}, f32[26,128]{1,0:T(8,128)S(1)}, u32[]{:S(2)}, u32[]{:S(2)}) %collective-permute-start.36) | collective-permute-done | bytes 13344 | tf_op jit(solution)/shard_map/ppermute | solution.py:39
  329.1 3.4 fusion.49
  339.5 2.4 collective-permute-start.39
  351.3 10.1 %collective-permute-done.53 = bf16[256,1024]{1,0:T(8,128)(2,1)} collective-permute-done((bf16[256,1024]{1,0:T(8,128)(2,1)}, bf16[256,1024]{1,0:T(8,128)(2,1)}, u32[]{:S(2)}, u32[]{:S(2)}) %collective-permute-start.53) | collective-permute-done | bytes 524320 | tf_op jit(solution)/shard_map/ppermute | solution.py:39
  368.2 5.4 %collective-permute-done.49 = bf16[256,1024]{0,1:T(8,128)(2,1)S(1)} collective-permute-done((bf16[256,1024]{0,1:T(8,128)(2,1)S(1)}, bf16[256,1024]{0,1:T(8,128)(2,1)S(1)}, u32[]{:S(2)}, u32[]{:S(2)}) %collective-permute-start.49) | collective-permute-done | bytes 524320 | tf_op jit(solution)/shard_map/ppermute | solution.py:39
  383.8 4.0 collective-permute-done.50
  389.5 2.4 collective-permute-start.51
  392.7 13.8 %collective-permute-done.51 = bf16[64,1024]{0,1:T(8,128)(2,1)S(1)} collective-permute-done((bf16[64,1024]{0,1:T(8,128)(2,1)S(1)}, bf16[64,1024]{0,1:T(8,128)(2,1)S(1)}, u32[]{:S(2)}, u32[]{:S(2)}) %collective-permute-start.51) | collective-permute-done | bytes 131104 | tf_op jit(solution)/shard_map/ppermute | solution.py:39
  419.8 2.5 collective-permute-start.63
  425.6 2.1 collective-permute-start.46
  428.4 2.1 collective-permute-done.63
  432.0 2.3 collective-permute-done.42
  439.2 2.3 collective-permute-done.43
  442.3 3.4 collective-permute-done.47
  (523 shorter events, 236.7 us)
Async XLA Ops:
  0.8 58.9 %collective-permute-start.19 = (bf16[64,1408]{1,0:T(8,128)(2,1)}, bf16[64,1408]{1,0:T(8,128)(2,1)S(1)}, u32[]{:S(2)}, u32[]{:S(2)}) collective-permute-start(bf16[64,1408]{1,0:T(8,128)(2,1)} %param.42), channel_id=1, source_target_pairs={{0,24},{2,26},{4,28},{6,30},{8,16},{10,18},{12,20},{14,22},{16,8},... | collective-permute-start | bytes 540680 | tf_op jit(solution)/shard_map/ppermute | solution.py:39
  5.9 54.6 %collective-permute-start.23 = (bf16[64,1408]{1,0:T(8,128)(2,1)}, bf16[64,1408]{1,0:T(8,128)(2,1)S(1)}, u32[]{:S(2)}, u32[]{:S(2)}) collective-permute-start(bf16[64,1408]{1,0:T(8,128)(2,1)} %param.43), channel_id=1, source_target_pairs={{0,24},{2,26},{4,28},{6,30},{8,16},{10,18},{12,20},{14,22},{16,8},... | collective-permute-start | bytes 540680 | tf_op jit(solution)/shard_map/ppermute | solution.py:39
  6.0 50.9 %collective-permute-start.27 = (bf16[64,1408]{1,0:T(8,128)(2,1)}, bf16[64,1408]{1,0:T(8,128)(2,1)S(1)}, u32[]{:S(2)}, u32[]{:S(2)}) collective-permute-start(bf16[64,1408]{1,0:T(8,128)(2,1)} %param.44), channel_id=1, source_target_pairs={{0,2},{2,0},{4,6},{6,4},{8,10},{10,8},{12,14},{14,12},{16,18},{18,... | collective-permute-start | bytes 540680 | tf_op jit(solution)/shard_map/ppermute | solution.py:39
  9.3 72.4 %all-to-all-start = ((bf16[16,8,1024]{2,1,0:T(8,128)(2,1)}), bf16[16,8,1024]{2,1,0:T(8,128)(2,1)}, u32[]{:S(2)}, u32[]{:S(2)}) async-start(bf16[16,8,1024]{2,1,0:T(8,128)(2,1)} %dynamic-slice_bitcast_fusion), calls=%async_computation | async-start | bytes 524288 | tf_op jit(solution)/shard_map/all_to_all | solution.py:273
  18.3 24.3 %collective-permute-start = (bf16[64,1024]{1,0:T(8,128)(2,1)}, bf16[64,1024]{1,0:T(8,128)(2,1)S(1)}, u32[]{:S(2)}, u32[]{:S(2)}) collective-permute-start(bf16[64,1024]{1,0:T(8,128)(2,1)} %get-tuple-element.146), channel_id=1, source_target_pairs={{0,24},{2,26},{4,28},{6,30},{8,16},{10,18},{12,20},{14,22},{16,8},... | collective-permute-start | bytes 393224 | tf_op jit(solution)/shard_map/ppermute | solution.py:39
  24.9 22.9 %collective-permute-start.4 = (bf16[64,1024]{1,0:T(8,128)(2,1)}, bf16[64,1024]{1,0:T(8,128)(2,1)S(1)}, u32[]{:S(2)}, u32[]{:S(2)}) collective-permute-start(bf16[64,1024]{1,0:T(8,128)(2,1)} %get-tuple-element.142), channel_id=1, source_target_pairs={{0,24},{2,26},{4,28},{6,30},{8,16},{10,18},{12,20},{14,22},{16,8},... | collective-permute-start | bytes 393224 | tf_op jit(solution)/shard_map/ppermute | solution.py:39
  50.0 15.7 %collective-permute-start.1 = (bf16[128,1024]{1,0:T(8,128)(2,1)S(1)}, bf16[128,1024]{1,0:T(8,128)(2,1)S(1)}, u32[]{:S(2)}, u32[]{:S(2)}) collective-permute-start(bf16[128,1024]{1,0:T(8,128)(2,1)S(1)} %pad_maximum_fusion.18), channel_id=1, source_target_pairs={{0,8},{2,10},{4,12},{6,14},{8,0},{10,2},{12,4},{14,6},{16,24},{18,... | collective-permute-start | bytes 786440 | tf_op jit(solution)/shard_map/ppermute | solution.py:39
  59.7 18.0 %collective-permute-start.15 = (bf16[128,1024]{1,0:T(8,128)(2,1)S(1)}, bf16[128,1024]{1,0:T(8,128)(2,1)S(1)}, u32[]{:S(2)}, u32[]{:S(2)}) collective-permute-start(bf16[128,1024]{1,0:T(8,128)(2,1)S(1)} %pad_maximum_fusion.21), channel_id=1, source_target_pairs={{0,8},{2,10},{4,12},{6,14},{8,0},{10,2},{12,4},{14,6},{16,24},{18,... | collective-permute-start | bytes 786440 | tf_op jit(solution)/shard_map/ppermute | solution.py:39
  60.5 34.6 %collective-permute-start.20 = (bf16[128,1408]{1,0:T(8,128)(2,1)}, bf16[128,1408]{1,0:T(8,128)(2,1)S(1)}, u32[]{:S(2)}, u32[]{:S(2)}) collective-permute-start(bf16[128,1408]{1,0:T(8,128)(2,1)} %pad_maximum_fusion.15), channel_id=1, source_target_pairs={{0,8},{2,10},{4,12},{6,14},{8,0},{10,2},{12,4},{14,6},{16,24},{18,... | collective-permute-start | bytes 1081352 | tf_op jit(solution)/shard_map/ppermute | solution.py:39
  65.6 32.8 %collective-permute-start.24 = (bf16[128,1408]{1,0:T(8,128)(2,1)}, bf16[128,1408]{1,0:T(8,128)(2,1)S(1)}, u32[]{:S(2)}, u32[]{:S(2)}) collective-permute-start(bf16[128,1408]{1,0:T(8,128)(2,1)} %pad_maximum_fusion.16), channel_id=1, source_target_pairs={{0,8},{2,10},{4,12},{6,14},{8,0},{10,2},{12,4},{14,6},{16,24},{18,... | collective-permute-start | bytes 1081352 | tf_op jit(solution)/shard_map/ppermute | solution.py:39
  68.2 23.0 %collective-permute-start.28 = (bf16[128,1408]{1,0:T(8,128)(2,1)}, bf16[128,1408]{1,0:T(8,128)(2,1)S(1)}, u32[]{:S(2)}, u32[]{:S(2)}) collective-permute-start(bf16[128,1408]{1,0:T(8,128)(2,1)} %pad_maximum_fusion.17), channel_id=1, source_target_pairs={{0,4},{2,6},{4,0},{6,2},{8,12},{10,14},{12,8},{14,10},{16,20},{18,... | collective-permute-start | bytes 1081352 | tf_op jit(solution)/shard_map/ppermute | solution.py:39
  72.1 30.4 %collective-permute-start.2 = (bf16[256,1024]{1,0:T(8,128)(2,1)}, bf16[256,1024]{1,0:T(8,128)(2,1)}, u32[]{:S(2)}, u32[]{:S(2)}) collective-permute-start(bf16[256,1024]{1,0:T(8,128)(2,1)} %pad_maximum_fusion.11), channel_id=1, source_target_pairs={{0,2},{2,0},{4,6},{6,4},{8,10},{10,8},{12,14},{14,12},{16,18},{18,... | collective-permute-start | bytes 1572872 | tf_op jit(solution)/shard_map/ppermute | solution.py:39
  77.7 26.9 %collective-permute-start.6 = (bf16[256,1024]{1,0:T(8,128)(2,1)}, bf16[256,1024]{1,0:T(8,128)(2,1)}, u32[]{:S(2)}, u32[]{:S(2)}) collective-permute-start(bf16[256,1024]{1,0:T(8,128)(2,1)} %pad_maximum_fusion.12), channel_id=1, source_target_pairs={{0,4},{2,6},{4,0},{6,2},{8,12},{10,14},{12,8},{14,10},{16,20},{18,... | collective-permute-start | bytes 1572872 | tf_op jit(solution)/shard_map/ppermute | solution.py:39
  85.7 28.7 %all-to-all-start.1 = ((bf16[16,8,1024]{2,1,0:T(8,128)(2,1)}), bf16[16,8,1024]{2,1,0:T(8,128)(2,1)}, u32[]{:S(2)}, u32[]{:S(2)}) async-start(bf16[16,8,1024]{2,1,0:T(8,128)(2,1)} %broadcast_select_fusion.1), calls=%async_computation.1 | async-start | bytes 524288 | tf_op jit(solution)/shard_map/all_to_all | solution.py:276
  91.2 25.2 %collective-permute-start.11 = (bf16[256,1024]{1,0:T(8,128)(2,1)}, bf16[256,1024]{1,0:T(8,128)(2,1)}, u32[]{:S(2)}, u32[]{:S(2)}) collective-permute-start(bf16[256,1024]{1,0:T(8,128)(2,1)} %pad_maximum_fusion.13), channel_id=1, source_target_pairs={{0,4},{2,6},{4,0},{6,2},{8,12},{10,14},{12,8},{14,10},{16,20},{18,... | collective-permute-start | bytes 1572872 | tf_op jit(solution)/shard_map/ppermute | solution.py:39
  95.1 17.4 %collective-permute-start.16 = (bf16[256,1024]{1,0:T(8,128)(2,1)}, bf16[256,1024]{1,0:T(8,128)(2,1)S(1)}, u32[]{:S(2)}, u32[]{:S(2)}) collective-permute-start(bf16[256,1024]{1,0:T(8,128)(2,1)} %pad_maximum_fusion.14), channel_id=1, source_target_pairs={{0,2},{2,0},{4,6},{6,4},{8,10},{10,8},{12,14},{14,12},{16,18},{18,... | collective-permute-start | bytes 1572872 | tf_op jit(solution)/shard_map/ppermute | solution.py:39
  98.4 26.0 %collective-permute-start.21 = (bf16[256,1408]{1,0:T(8,128)(2,1)}, bf16[256,1408]{1,0:T(8,128)(2,1)}, u32[]{:S(2)}, u32[]{:S(2)}) collective-permute-start(bf16[256,1408]{1,0:T(8,128)(2,1)} %pad_maximum_fusion.8), channel_id=1, source_target_pairs={{0,2},{2,0},{4,6},{6,4},{8,10},{10,8},{12,14},{14,12},{16,18},{18,... | collective-permute-start | bytes 2162696 | tf_op jit(solution)/shard_map/ppermute | solution.py:39
  102.5 23.9 %collective-permute-start.25 = (bf16[256,1408]{1,0:T(8,128)(2,1)}, bf16[256,1408]{1,0:T(8,128)(2,1)}, u32[]{:S(2)}, u32[]{:S(2)}) collective-permute-start(bf16[256,1408]{1,0:T(8,128)(2,1)} %pad_maximum_fusion.9), channel_id=1, source_target_pairs={{0,4},{2,6},{4,0},{6,2},{8,12},{10,14},{12,8},{14,10},{16,20},{18,... | collective-permute-start | bytes 2162696 | tf_op jit(solution)/shard_map/ppermute | solution.py:39
  104.6 17.9 %collective-permute-start.29 = (bf16[256,1408]{1,0:T(8,128)(2,1)}, bf16[256,1408]{1,0:T(8,128)(2,1)}, u32[]{:S(2)}, u32[]{:S(2)}) collective-permute-start(bf16[256,1408]{1,0:T(8,128)(2,1)} %pad_maximum_fusion.10), channel_id=1, source_target_pairs={{0,24},{2,26},{4,28},{6,30},{8,16},{10,18},{12,20},{14,22},{16,8},... | collective-permute-start | bytes 2162696 | tf_op jit(solution)/shard_map/ppermute | solution.py:39
  116.4 26.2 %collective-permute-start.3 = (bf16[512,1024]{1,0:T(8,128)(2,1)}, bf16[512,1024]{1,0:T(8,128)(2,1)S(1)}, u32[]{:S(2)}, u32[]{:S(2)}) collective-permute-start(bf16[512,1024]{1,0:T(8,128)(2,1)} %pad_maximum_fusion.4), channel_id=1, source_target_pairs={{0,4},{2,6},{4,0},{6,2},{8,12},{10,14},{12,8},{14,10},{16,20},{18,... | collective-permute-start | bytes 3145736 | tf_op jit(solution)/shard_map/ppermute | solution.py:39
  119.0 27.7 %collective-permute-start.7 = (bf16[512,1024]{1,0:T(8,128)(2,1)S(1)}, bf16[512,1024]{1,0:T(8,128)(2,1)S(1)}, u32[]{:S(2)}, u32[]{:S(2)}) collective-permute-start(bf16[512,1024]{1,0:T(8,128)(2,1)S(1)} %copy-done.68), channel_id=1, source_target_pairs={{0,2},{2,0},{4,6},{6,4},{8,10},{10,8},{12,14},{14,12},{16,18},{18,... | collective-permute-start | bytes 3145736 | tf_op jit(solution)/shard_map/ppermute | solution.py:39
  122.6 45.0 %collective-permute-start.12 = (bf16[512,1024]{1,0:T(8,128)(2,1)S(1)}, bf16[512,1024]{1,0:T(8,128)(2,1)S(1)}, u32[]{:S(2)}, u32[]{:S(2)}) collective-permute-start(bf16[512,1024]{1,0:T(8,128)(2,1)S(1)} %pad_maximum_fusion.6), channel_id=1, source_target_pairs={{0,2},{2,0},{4,6},{6,4},{8,10},{10,8},{12,14},{14,12},{16,18},{18,... | collective-permute-start | bytes 3145736 | tf_op jit(solution)/shard_map/ppermute | solution.py:39
  124.5 40.6 %collective-permute-start.17 = (bf16[512,1024]{1,0:T(8,128)(2,1)S(1)}, bf16[512,1024]{1,0:T(8,128)(2,1)S(1)}, u32[]{:S(2)}, u32[]{:S(2)}) collective-permute-start(bf16[512,1024]{1,0:T(8,128)(2,1)S(1)} %copy-done.67), channel_id=1, source_target_pairs={{0,4},{2,6},{4,0},{6,2},{8,12},{10,14},{12,8},{14,10},{16,20},{18,... | collective-permute-start | bytes 3145736 | tf_op jit(solution)/shard_map/ppermute | solution.py:39
  126.3 69.1 %collective-permute-start.22 = (bf16[512,1408]{1,0:T(8,128)(2,1)S(1)}, bf16[512,1408]{1,0:T(8,128)(2,1)S(1)}, u32[]{:S(2)}, u32[]{:S(2)}) collective-permute-start(bf16[512,1408]{1,0:T(8,128)(2,1)S(1)} %pad_maximum_fusion), channel_id=1, source_target_pairs={{0,4},{2,6},{4,0},{6,2},{8,12},{10,14},{12,8},{14,10},{16,20},{18,... | collective-permute-start | bytes 4325384 | tf_op jit(solution)/shard_map/ppermute | solution.py:39
  142.5 55.2 %collective-permute-start.26 = (bf16[512,1408]{1,0:T(8,128)(2,1)S(1)}, bf16[512,1408]{1,0:T(8,128)(2,1)S(1)}, u32[]{:S(2)}, u32[]{:S(2)}) collective-permute-start(bf16[512,1408]{1,0:T(8,128)(2,1)S(1)} %pad_maximum_fusion.1), channel_id=1, source_target_pairs={{0,2},{2,0},{4,6},{6,4},{8,10},{10,8},{12,14},{14,12},{16,18},{18,... | collective-permute-start | bytes 4325384 | tf_op jit(solution)/shard_map/ppermute | solution.py:39
  146.7 32.4 %collective-permute-start.30 = (bf16[512,1408]{1,0:T(8,128)(2,1)S(1)}, bf16[512,1408]{1,0:T(8,128)(2,1)S(1)}, u32[]{:S(2)}, u32[]{:S(2)}) collective-permute-start(bf16[512,1408]{1,0:T(8,128)(2,1)S(1)} %pad_maximum_fusion.2), channel_id=1, source_target_pairs={{0,8},{2,10},{4,12},{6,14},{8,0},{10,2},{12,4},{14,6},{16,24},{18,... | collective-permute-start | bytes 4325384 | tf_op jit(solution)/shard_map/ppermute | solution.py:39
  174.6 27.0 %collective-permute-start.18 = (bf16[256,1024]{0,1:T(8,128)(2,1)S(1)}, bf16[256,1024]{0,1:T(8,128)(2,1)S(1)}, u32[]{:S(2)}, u32[]{:S(2)}) collective-permute-start(bf16[256,1024]{0,1:T(8,128)(2,1)S(1)} %convolution_convert_fusion.11), channel_id=1, source_target_pairs={{0,1},{1,0},{2,3},{3,2},{4,5},{5,4},{6,7},{7,6},{8,9},{9,8},{10,11... | collective-permute-start | bytes 1572872 | tf_op jit(solution)/shard_map/ppermute | solution.py:43
  219.6 27.4 %collective-permute-start.31 = (bf16[256,1024]{0,1:T(8,128)(2,1)S(1)}, bf16[256,1024]{0,1:T(8,128)(2,1)S(1)}, u32[]{:S(2)}, u32[]{:S(2)}) collective-permute-start(bf16[256,1024]{0,1:T(8,128)(2,1)S(1)} %convolution_convert_fusion.13), channel_id=1, source_target_pairs={{0,1},{1,0},{2,3},{3,2},{4,5},{5,4},{6,7},{7,6},{8,9},{9,8},{10,11... | collective-permute-start | bytes 1572872 | tf_op jit(solution)/shard_map/ppermute | solution.py:43
  221.3 72.6 %collective-permute-start.56 = (bf16[512,1408]{1,0:T(8,128)(2,1)}, bf16[512,1408]{1,0:T(8,128)(2,1)}, u32[]{:S(2)}, u32[]{:S(2)}) collective-permute-start(bf16[512,1408]{1,0:T(8,128)(2,1)} %slice.632), channel_id=1, source_target_pairs={{0,4},{2,6},{4,0},{6,2},{8,12},{10,14},{12,8},{14,10},{16,20},{18,... | collective-permute-start | bytes 4325384 | tf_op jit(solution)/shard_map/ppermute | solution.py:39
  225.4 72.9 %collective-permute-start.60 = (bf16[512,1408]{1,0:T(8,128)(2,1)}, bf16[512,1408]{1,0:T(8,128)(2,1)}, u32[]{:S(2)}, u32[]{:S(2)}) collective-permute-start(bf16[512,1408]{1,0:T(8,128)(2,1)} %pad_maximum_fusion.3), channel_id=1, source_target_pairs={{0,2},{2,0},{4,6},{6,4},{8,10},{10,8},{12,14},{14,12},{16,18},{18,... | collective-permute-start | bytes 4325384 | tf_op jit(solution)/shard_map/ppermute | solution.py:39
  232.5 70.5 %collective-permute-start.64 = (bf16[512,1408]{1,0:T(8,128)(2,1)}, bf16[512,1408]{1,0:T(8,128)(2,1)}, u32[]{:S(2)}, u32[]{:S(2)}) collective-permute-start(bf16[512,1408]{1,0:T(8,128)(2,1)} %get-tuple-element.98), channel_id=1, source_target_pairs={{0,8},{2,10},{4,12},{6,14},{8,0},{10,2},{12,4},{14,6},{16,24},{18,... | collective-permute-start | bytes 4325384 | tf_op jit(solution)/shard_map/ppermute | solution.py:39
  249.6 84.6 %collective-permute-start.52 = (bf16[512,1024]{1,0:T(8,128)(2,1)}, bf16[512,1024]{1,0:T(8,128)(2,1)}, u32[]{:S(2)}, u32[]{:S(2)}) collective-permute-start(bf16[512,1024]{1,0:T(8,128)(2,1)} %slice.620), channel_id=1, source_target_pairs={{0,4},{2,6},{4,0},{6,2},{8,12},{10,14},{12,8},{14,10},{16,20},{18,... | collective-permute-start | bytes 3145736 | tf_op jit(solution)/shard_map/ppermute | solution.py:39
  251.9 34.9 %all-to-all-start.2 = ((bf16[16,8,1024]{2,1,0:T(8,128)(2,1)}), bf16[16,8,1024]{2,1,0:T(8,128)(2,1)S(1)}, u32[]{:S(2)}, u32[]{:S(2)}) async-start(bf16[16,8,1024]{2,1,0:T(8,128)(2,1)} %fusion.51), calls=%async_computation.2 | async-start | bytes 524288 | tf_op jit(solution)/shard_map/all_to_all | solution.py:273
  256.1 83.5 %collective-permute-start.48 = (bf16[512,1024]{0,1:T(8,128)(2,1)}, bf16[512,1024]{0,1:T(8,128)(2,1)}, u32[]{:S(2)}, u32[]{:S(2)}) collective-permute-start(bf16[512,1024]{0,1:T(8,128)(2,1)} %fusion.55), channel_id=1, source_target_pairs={{0,2},{2,0},{4,6},{6,4},{8,10},{10,8},{12,14},{14,12},{16,18},{18,... | collective-permute-start | bytes 3145736 | tf_op jit(solution)/shard_map/ppermute | solution.py:39
  288.1 59.7 %all-to-all-start.3 = ((bf16[16,8,1024]{2,1,0:T(8,128)(2,1)}), bf16[16,8,1024]{2,1,0:T(8,128)(2,1)S(1)}, u32[]{:S(2)}, u32[]{:S(2)}) async-start(bf16[16,8,1024]{2,1,0:T(8,128)(2,1)} %broadcast_select_fusion), calls=%async_computation.3 | async-start | bytes 524288 | tf_op jit(solution)/shard_map/all_to_all | solution.py:276
  298.4 49.5 %collective-permute-start.40 = (bf16[512,1024]{1,0:T(8,128)(2,1)}, bf16[512,1024]{1,0:T(8,128)(2,1)}, u32[]{:S(2)}, u32[]{:S(2)}) collective-permute-start(bf16[512,1024]{1,0:T(8,128)(2,1)} %slice.582), channel_id=1, source_target_pairs={{0,4},{2,6},{4,0},{6,2},{8,12},{10,14},{12,8},{14,10},{16,20},{18,... | collective-permute-start | bytes 3145736 | tf_op jit(solution)/shard_map/ppermute | solution.py:39
  303.0 62.1 %collective-permute-start.44 = (bf16[512,1024]{0,1:T(8,128)(2,1)}, bf16[512,1024]{0,1:T(8,128)(2,1)}, u32[]{:S(2)}, u32[]{:S(2)}) collective-permute-start(bf16[512,1024]{0,1:T(8,128)(2,1)} %fusion.53), channel_id=1, source_target_pairs={{0,2},{2,0},{4,6},{6,4},{8,10},{10,8},{12,14},{14,12},{16,18},{18,... | collective-permute-start | bytes 3145736 | tf_op jit(solution)/shard_map/ppermute | solution.py:39
  311.5 17.3 %collective-permute-start.36 = (f32[26,128]{1,0:T(8,128)S(1)}, f32[26,128]{1,0:T(8,128)S(1)}, u32[]{:S(2)}, u32[]{:S(2)}) collective-permute-start(f32[26,128]{1,0:T(8,128)S(1)} %maximum_bitcast_fusion), channel_id=1, source_target_pairs={{0,2},{2,0},{4,6},{6,4},{8,10},{10,8},{12,14},{14,12},{16,18},{18,... | collective-permute-start | bytes 39944 | tf_op jit(solution)/shard_map/ppermute | solution.py:39
  332.5 43.6 %collective-permute-start.57 = (bf16[256,1408]{1,0:T(8,128)(2,1)}, bf16[256,1408]{1,0:T(8,128)(2,1)S(1)}, u32[]{:S(2)}, u32[]{:S(2)}) collective-permute-start(bf16[256,1408]{1,0:T(8,128)(2,1)} %slice.830), channel_id=1, source_target_pairs={{0,2},{2,0},{4,6},{6,4},{8,10},{10,8},{12,14},{14,12},{16,18},{18,... | collective-permute-start | bytes 2162696 | tf_op jit(solution)/shard_map/ppermute | solution.py:39
  338.1 40.5 %collective-permute-start.61 = (bf16[256,1408]{1,0:T(8,128)(2,1)}, bf16[256,1408]{1,0:T(8,128)(2,1)}, u32[]{:S(2)}, u32[]{:S(2)}) collective-permute-start(bf16[256,1408]{1,0:T(8,128)(2,1)} %slice.829), channel_id=1, source_target_pairs={{0,4},{2,6},{4,0},{6,2},{8,12},{10,14},{12,8},{14,10},{16,20},{18,... | collective-permute-start | bytes 2162696 | tf_op jit(solution)/shard_map/ppermute | solution.py:39
  345.9 15.5 %collective-permute-start.53 = (bf16[256,1024]{1,0:T(8,128)(2,1)}, bf16[256,1024]{1,0:T(8,128)(2,1)}, u32[]{:S(2)}, u32[]{:S(2)}) collective-permute-start(bf16[256,1024]{1,0:T(8,128)(2,1)} %slice.831), channel_id=1, source_target_pairs={{0,2},{2,0},{4,6},{6,4},{8,10},{10,8},{12,14},{14,12},{16,18},{18,... | collective-permute-start | bytes 1572872 | tf_op jit(solution)/shard_map/ppermute | solution.py:39
  347.9 33.5 %collective-permute-start.65 = (bf16[256,1408]{1,0:T(8,128)(2,1)}, bf16[256,1408]{1,0:T(8,128)(2,1)S(1)}, u32[]{:S(2)}, u32[]{:S(2)}) collective-permute-start(bf16[256,1408]{1,0:T(8,128)(2,1)} %slice.828), channel_id=1, source_target_pairs={{0,24},{2,26},{4,28},{6,30},{8,16},{10,18},{12,20},{14,22},{16,8},... | collective-permute-start | bytes 2162696 | tf_op jit(solution)/shard_map/ppermute | solution.py:39
  365.1 24.4 %collective-permute-start.54 = (bf16[128,1024]{1,0:T(8,128)(2,1)S(1)}, bf16[128,1024]{1,0:T(8,128)(2,1)S(1)}, u32[]{:S(2)}, u32[]{:S(2)}) collective-permute-start(bf16[128,1024]{1,0:T(8,128)(2,1)S(1)} %slice.838), channel_id=1, source_target_pairs={{0,8},{2,10},{4,12},{6,14},{8,0},{10,2},{12,4},{14,6},{16,24},{18,... | collective-permute-start | bytes 786440 | tf_op jit(solution)/shard_map/ppermute | solution.py:39
  373.6 49.3 %collective-permute-start.41 = (bf16[256,1024]{1,0:T(8,128)(2,1)}, bf16[256,1024]{1,0:T(8,128)(2,1)}, u32[]{:S(2)}, u32[]{:S(2)}) collective-permute-start(bf16[256,1024]{1,0:T(8,128)(2,1)} %slice.834), channel_id=1, source_target_pairs={{0,2},{2,0},{4,6},{6,4},{8,10},{10,8},{12,14},{14,12},{16,18},{18,... | collective-permute-start | bytes 1572872 | tf_op jit(solution)/shard_map/ppermute | solution.py:39
  376.1 48.2 %collective-permute-start.45 = (bf16[256,1024]{0,1:T(8,128)(2,1)}, bf16[256,1024]{0,1:T(8,128)(2,1)}, u32[]{:S(2)}, u32[]{:S(2)}) collective-permute-start(bf16[256,1024]{0,1:T(8,128)(2,1)} %slice.833), channel_id=1, source_target_pairs={{0,4},{2,6},{4,0},{6,2},{8,12},{10,14},{12,8},{14,10},{16,20},{18,... | collective-permute-start | bytes 1572872 | tf_op jit(solution)/shard_map/ppermute | solution.py:39
  381.3 34.6 %collective-permute-start.58 = (bf16[128,1408]{1,0:T(8,128)(2,1)}, bf16[128,1408]{1,0:T(8,128)(2,1)}, u32[]{:S(2)}, u32[]{:S(2)}) collective-permute-start(bf16[128,1408]{1,0:T(8,128)(2,1)} %slice.837), channel_id=1, source_target_pairs={{0,8},{2,10},{4,12},{6,14},{8,0},{10,2},{12,4},{14,6},{16,24},{18,... | collective-permute-start | bytes 1081352 | tf_op jit(solution)/shard_map/ppermute | solution.py:39
  387.8 30.9 %collective-permute-start.62 = (bf16[128,1408]{1,0:T(8,128)(2,1)}, bf16[128,1408]{1,0:T(8,128)(2,1)}, u32[]{:S(2)}, u32[]{:S(2)}) collective-permute-start(bf16[128,1408]{1,0:T(8,128)(2,1)} %slice.836), channel_id=1, source_target_pairs={{0,8},{2,10},{4,12},{6,14},{8,0},{10,2},{12,4},{14,6},{16,24},{18,... | collective-permute-start | bytes 1081352 | tf_op jit(solution)/shard_map/ppermute | solution.py:39
  389.5 17.0 %collective-permute-start.51 = (bf16[64,1024]{0,1:T(8,128)(2,1)S(1)}, bf16[64,1024]{0,1:T(8,128)(2,1)S(1)}, u32[]{:S(2)}, u32[]{:S(2)}) collective-permute-start(bf16[64,1024]{0,1:T(8,128)(2,1)S(1)} %slice.839), channel_id=1, source_target_pairs={{0,24},{2,26},{4,28},{6,30},{8,16},{10,18},{12,20},{14,22},{16,8},... | collective-permute-start | bytes 393224 | tf_op jit(solution)/shard_map/ppermute | solution.py:39
  (115 other events, 1453.9 us)
